TPU v7x, 256 devices: a whole 4x4x8 slice. The times are simulated.
256 devices in a mesh: dp: 16 (over x, y_hi, core), expert: 16 (over y_lo, z).
Axes of the slice: x: 4, y: 4 (y_hi: 2, y_lo: 2; y = y_hi * 2 + y_lo), z: 8, core: 2. Of those that a mesh axis runs over, the one named last changes fastest.
Arguments:
- tokens: bfloat16 [2048, 7168], P('dp', 'expert'), may hold values from -6 to 6
- grad_out: bfloat16 [2048, 7168], P('dp', 'expert'), may hold values from -6 to 6
- w_gate: bfloat16 [16, 7168, 2048], P('dp', None, 'expert'), may hold values from -0.0625 to 0.0625
- w_up: bfloat16 [16, 7168, 2048], P('dp', None, 'expert'), may hold values from -0.0625 to 0.0625
- w_down: bfloat16 [16, 2048, 7168], P('dp', 'expert'), may hold values from -0.125 to 0.125
- routing: int32 [2048, 2], replicated, may hold values from 0 to 15, as said below
- combine: float32 [2048, 2], replicated, may hold values from 0.2 to 1
- hot_ids: int32 [16], replicated, may hold values from 0 to 15, as said below
Outputs:
- grad_gate: bfloat16 [16, 7168, 2048], P('dp', None, 'expert')
- grad_up: bfloat16 [16, 7168, 2048], P('dp', None, 'expert')
- grad_down: bfloat16 [16, 2048, 7168], P('dp', 'expert')
- grad_tokens: bfloat16 [2048, 7168], P('dp', 'expert')
Inputs may be any that keep to these rules, and one draw needn't show every extreme that they name: `routing`: each token names 2 different experts. `hot_ids`: a permutation of the 16 experts.
All inputs are finite; a program needn't handle non-finite values.
Results may differ from a plain program's by a relative error of at most 0.018.
Values may be sent and summed in bfloat16 or wider, within the bound.
A program may use at most 128 MiB of HBM per device.

v0:
```python
import jax
import jax.numpy as jnp
from jax import lax
from jax.sharding import PartitionSpec as P


def broadcast(block, axis, owner):
    block = jnp.where(lax.axis_index(axis) == owner, block, jnp.zeros_like(block))
    return lax.psum(block, axis)


def slot_tables(routing, combine, hot_expert, dp_count, block_rows, expert_count, capacity):
    columns = jnp.arange(expert_count, dtype=jnp.int32)
    name_match = routing[:, :, None] == columns[None, None, :]
    route_weight = jnp.sum(jnp.where(name_match, combine[:, :, None], jnp.float32(0.0)), axis=1)
    named_count = jnp.sum(name_match.astype(jnp.int32), axis=1).reshape(
        dp_count, block_rows, expert_count
    )
    before = jnp.cumsum(named_count, axis=1) - named_count
    slot_ids = jnp.arange(capacity, dtype=jnp.int32)
    slot_match = (
        (named_count[..., None] == 1)
        & (before[..., None] == slot_ids)
        & (columns != hot_expert)[None, None, :, None]
    )
    positions = jnp.arange(block_rows, dtype=jnp.int32)
    slot_token = jnp.sum(jnp.where(slot_match, positions[None, :, None, None], 0), axis=1)
    slot_live = jnp.any(slot_match, axis=1)
    return (route_weight, slot_token, slot_live)


def expert_terms(rows_in, rows_back, weight, gate_cols, up_cols, down_rows):
    across = (((1,), (1,)), ((), ()))
    downward = (((0,), (0,)), ((), ()))
    gate_pre = jnp.dot(rows_in, gate_cols, preferred_element_type=jnp.float32)
    up_pre = jnp.dot(rows_in, up_cols, preferred_element_type=jnp.float32)
    sigmoid_gate = jax.nn.sigmoid(gate_pre)
    active = gate_pre * sigmoid_gate
    back_hidden = weight[:, None] * lax.dot_general(
        rows_back, down_rows, across, preferred_element_type=jnp.float32
    )
    scaled = (weight[:, None] * active * up_pre).astype(jnp.bfloat16)
    grad_gate_pre = (
        back_hidden * up_pre * sigmoid_gate * (1.0 + gate_pre * (1.0 - sigmoid_gate))
    ).astype(jnp.bfloat16)
    grad_up_pre = (back_hidden * active).astype(jnp.bfloat16)
    gate_sum = lax.dot_general(rows_in, grad_gate_pre, downward, preferred_element_type=jnp.float32)
    up_sum = lax.dot_general(rows_in, grad_up_pre, downward, preferred_element_type=jnp.float32)
    down_sum = lax.dot_general(scaled, rows_back, downward, preferred_element_type=jnp.float32)
    back = lax.dot_general(grad_gate_pre, gate_cols, across, preferred_element_type=jnp.float32)
    back = back + lax.dot_general(grad_up_pre, up_cols, across, preferred_element_type=jnp.float32)
    return (gate_sum, up_sum, down_sum, back)


def on_device(tokens, grad_out, w_gate, w_up, w_down, routing, combine, hot_ids):
    dp_count = lax.axis_size("dp")
    block_rows = tokens.shape[0]
    share_width = tokens.shape[1]
    top_count = routing.shape[1]
    capacity = block_rows * top_count // dp_count
    row_index = lax.axis_index("dp")
    hot_expert = hot_ids[0]
    route_weight, slot_token, slot_live = slot_tables(
        routing, combine, hot_expert, dp_count, block_rows, dp_count, capacity
    )
    send_token = slot_token[row_index]
    send_live = slot_live[row_index]
    recv_token = (
        slot_token[:, row_index, :] + (jnp.arange(dp_count, dtype=jnp.int32) * block_rows)[:, None]
    )
    recv_live = slot_live[:, row_index, :]
    cold_weight = jnp.where(
        recv_live, route_weight[recv_token, row_index], jnp.float32(0.0)
    ).reshape(-1)
    block_weight = lax.dynamic_slice_in_dim(route_weight, row_index * block_rows, block_rows, 0)
    hot_weight = block_weight[:, hot_expert]
    hot_gate_w, hot_up_w, hot_down_w = (
        broadcast(w_gate[0], "dp", hot_expert),
        broadcast(w_up[0], "dp", hot_expert),
        broadcast(w_down[0], "dp", hot_expert),
    )

    def pack(source):
        picked = jnp.take(source, send_token.reshape(-1), axis=0).reshape(
            dp_count, capacity, source.shape[1]
        )
        return jnp.where(send_live[:, :, None], picked, jnp.zeros_like(picked))

    arrived_in, arrived_back = (
        lax.all_to_all(pack(tokens), "dp", split_axis=0, concat_axis=0, tiled=True),
        lax.all_to_all(pack(grad_out), "dp", split_axis=0, concat_axis=0, tiled=True),
    )
    local_in = jnp.concatenate([tokens, arrived_in.reshape(-1, share_width)], 0)
    local_back = jnp.concatenate([grad_out, arrived_back.reshape(-1, share_width)], 0)
    full_in, full_back = (
        lax.all_gather(local_in, "expert", axis=1, tiled=True),
        lax.all_gather(local_back, "expert", axis=1, tiled=True),
    )
    hot_rows, cold_rows = (full_in[:block_rows], full_in[block_rows:])
    hot_cotan, cold_cotan = (full_back[:block_rows], full_back[block_rows:])
    hot_terms = expert_terms(hot_rows, hot_cotan, hot_weight, hot_gate_w, hot_up_w, hot_down_w)
    cold_terms = expert_terms(cold_rows, cold_cotan, cold_weight, w_gate[0], w_up[0], w_down[0])
    summed = (
        lax.psum(hot_terms[0].astype(jnp.bfloat16), "dp").astype(jnp.float32),
        lax.psum(hot_terms[1].astype(jnp.bfloat16), "dp").astype(jnp.float32),
        lax.psum(hot_terms[2].astype(jnp.bfloat16), "dp").astype(jnp.float32),
    )
    owns_hot = row_index == hot_expert
    expert_grads = tuple(
        (
            jnp.where(owns_hot, summed[member], cold_terms[member]).astype(jnp.bfloat16)[None]
            for member in range(3)
        )
    )
    positions = jnp.arange(block_rows, dtype=jnp.int32)
    select = (positions[:, None] == send_token.reshape(-1)[None, :]) & send_live.reshape(-1)[
        None, :
    ]
    stacked = jnp.concatenate([hot_terms[3], cold_terms[3]], 0)
    shares = lax.psum_scatter(
        stacked.astype(jnp.bfloat16), "expert", scatter_dimension=1, tiled=True
    ).astype(jnp.float32)
    hot_share = shares[:block_rows]
    cold_share = shares[block_rows:].reshape(dp_count, capacity, share_width)
    returned = lax.all_to_all(
        cold_share.astype(jnp.bfloat16), "dp", split_axis=0, concat_axis=0, tiled=True
    ).astype(cold_share.dtype)
    gathered_back = jnp.dot(
        select.astype(jnp.float32),
        returned.reshape(-1, share_width),
        precision=lax.Precision.HIGHEST,
        preferred_element_type=jnp.float32,
    )
    token_grad = (hot_share + gathered_back).astype(jnp.bfloat16)
    return (expert_grads[0], expert_grads[1], expert_grads[2], token_grad)


def solution(mesh):
    return jax.shard_map(
        on_device,
        mesh=mesh,
        in_specs=(
            P("dp", "expert"),
            P("dp", "expert"),
            P("dp", None, "expert"),
            P("dp", None, "expert"),
            P("dp", "expert", None),
            P(),
            P(),
            P(),
        ),
        out_specs=(
            P("dp", None, "expert"),
            P("dp", None, "expert"),
            P("dp", "expert", None),
            P("dp", "expert"),
        ),
        check_vma=False,
    )
```

profile of v0, /device:TPU:1, one launch (start us, length us, event | category | flops | bytes accessed | tf_op | source)
XLA Modules:
  0.0 552.7 jit_solution(17194985707236843325)
XLA Ops:
  8.0 0.0 all-reduce.8.cloned.1.call-start
  8.7 3.0 bitcast_select_fusion.2
  11.7 2.1 bitcast_select_fusion
  13.8 0.0 all-reduce.8.cloned.1.call-update
  13.8 0.0 all-gather.3.cloned.1.call-start
  13.9 0.8 copy-done.5
  14.7 0.1 copy.75
  14.8 0.1 copy.78
  15.1 0.5 copy.71
  15.6 23.3 %fusion.59 = s32[16,128,16]{2,0,1:T(8,128)S(1)} fusion(s32[16,128,16]{2,0,1:T(8,128)S(1)} %copy.71), kind=kOutput, calls=%fused_computation.99 | output fusion | flops 4161536 | bytes 262144 | tf_op jit(solution)/shard_map/jit(cumsum)/reduce_window_sum | solution.py:19
  38.9 1.1 sub.13
  40.0 1.6 copy.73
  41.7 4.5 select_reduce_fusion
  46.2 0.1 reshape_squeeze.4
  46.3 1.2 gather_fusion.2
  47.5 1.2 gather_fusion.1
  48.6 4.6 fusion.25
  53.2 0.1 broadcast_select_fusion
  53.3 0.1 broadcast_select_fusion.2
  53.5 18.0 %all_to_all.15 = bf16[16,16,448]{2,1,0:T(8,128)(2,1)S(1)} all-to-all(bf16[16,16,448]{2,1,0:T(8,128)(2,1)S(1)} %get-tuple-element.28), channel_id=1, replica_groups=mesh['dp'=16,'expert'=16] {'dp'}, dimensions={0} | all-to-all | bytes 458752 | tf_op jit(solution)/shard_map/all_to_all | solution.py:90
  71.5 0.9 copy.76
  72.4 0.0 all-gather.3.cloned.1.call-update
  72.5 0.0 all-gather.5.cloned.1.call-start
  72.5 14.7 %all_to_all.16 = bf16[16,16,448]{2,1,0:T(8,128)(2,1)S(1)} all-to-all(bf16[16,16,448]{2,1,0:T(8,128)(2,1)S(1)} %get-tuple-element.27), channel_id=1, replica_groups=mesh['dp'=16,'expert'=16] {'dp'}, dimensions={0} | all-to-all | bytes 458752 | tf_op jit(solution)/shard_map/all_to_all | solution.py:91
  87.2 0.9 copy.79
  88.2 0.0 all-gather.5.cloned.1.call-update
  88.2 0.2 all-reduce.6.cloned.1.call-start
  88.6 0.1 dynamic-slice_bitcast_fusion
  88.7 202.1 %all-reduce.8.cloned.1.call-done = (bf16[7168,128]{1,0:T(8,128)(2,1)}, bf16[128,7168]{1,0:T(8,128)(2,1)}, bf16[7168,128]{1,0:T(8,128)(2,1)}) async-done(((bf16[7168,128]{1,0:T(8,128)(2,1)}, bf16[128,7168]{1,0:T(8,128)(2,1)}, bf16[7168,128]{1,0:T(8,128)(2,1)}), (bf16[7168,128]{1,0:T(8,128)(2,1)}, bf16[128,7168]{1,0:T(8,128)(2,1)}, bf16[7168,128]{1,0:T(8,128)(2,1)})) %all-reduce.8.cloned.1.call-update) | async-done | bytes 5505040 | tf_op jit(solution)/shard_map/psum | solution.py:9
  290.8 2.9 fusion.31
  293.7 2.2 fusion.33
  295.9 0.0 all-gather.5.cloned.1.call-done
  295.9 3.6 convolution_convert_fusion
  299.5 2.2 multiply_convert_fusion.5
  301.8 3.4 convolution_convert_fusion.1
  305.1 3.3 convolution_convert_fusion.2
  308.5 0.0 all-reduce.6.cloned.1.call-update
  308.5 0.0 reduce-scatter.4.cloned.1.call-start
  308.6 0.1 squeeze.25
  308.7 0.1 fusion.56
  308.8 0.1 reshape.133
  308.9 2.4 gather_fusion
  311.3 2.3 fusion.60
  313.6 2.3 fusion.4
  316.0 1.2 fusion.13
  317.2 1.2 fusion.15
  318.4 0.0 slice-done.5
  318.4 0.8 copy-done.4
  319.2 1.2 multiply_convert_fusion.1
  320.4 1.1 fusion.19
  321.5 1.2 fusion
  322.7 2.8 pad_maximum_fusion
  325.5 8.3 %copy.81 = bf16[384,7168]{0,1:T(8,128)(2,1)} copy(bf16[384,7168]{1,0:T(8,128)(2,1)} %pad_maximum_fusion) | data formatting | bytes 11010048
  333.7 0.0 reduce-scatter.4.cloned.1.call-update
  333.8 0.1 and.35
  333.9 183.6 %all-reduce.6.cloned.1.call-done = (bf16[7168,128]{1,0:T(8,128)(2,1)}, bf16[7168,128]{1,0:T(8,128)(2,1)}, bf16[128,7168]{1,0:T(8,128)(2,1)}) async-done(((bf16[7168,128]{1,0:T(8,128)(2,1)}, bf16[7168,128]{1,0:T(8,128)(2,1)}, bf16[128,7168]{1,0:T(8,128)(2,1)}), (bf16[7168,128]{1,0:T(8,128)(2,1)}, bf16[7168,128]{1,0:T(8,128)(2,1)}, bf16[128,7168]{1,0:T(8,128)(2,1)})) %all-reduce.6.cloned.1.call-update) | async-done | bytes 5505040 | tf_op jit(solution)/shard_map/psum | solution.py:104
  517.5 5.1 fusion.7
  522.6 2.4 fusion.6
  525.0 1.0 slice.44
  525.9 0.8 copy.83
  526.8 7.6 %all-to-all-start.2 = ((bf16[16,16,448]{2,1,0:T(8,128)(2,1)}), bf16[16,16,448]{2,1,0:T(8,128)(2,1)S(1)}, u32[]{:S(2)}, u32[]{:S(2)}) async-start(bf16[16,16,448]{2,1,0:T(8,128)(2,1)} %bitcast.14), calls=%async_computation.2 | async-start | bytes 524288 | tf_op jit(solution)/shard_map/all_to_all | solution.py:125
  534.4 5.3 fusion.5
  539.7 3.6 all-to-all-done.2
  543.3 1.8 fusion.35
  (58 shorter events, 0.4 us)
Async XLA Ops:
  8.0 282.8 %all-reduce.8.cloned.1.call-start = ((), (), s32[]{:S(2)}) async-start(), calls=%async_computation.8 | async-start | bytes 11010048 | tf_op jit(solution)/shard_map/psum | solution.py:9
  8.7 3.0 copy-start
  8.7 3.0 copy-start.1
  13.8 0.9 copy-start.5
  13.8 1.0 copy-start.6
  13.8 1.1 copy-start.7
  13.8 277.0 %all-gather.3.cloned.1.call-start = ((), (), s32[]{:S(2)}) async-start(), calls=%async_computation.4 | async-start | bytes 5849088 | tf_op jit(solution)/shard_map/all_gather | solution.py:96
  38.9 2.8 copy-start.9
  71.5 17.0 %copy-start.8 = (f32[2048,2]{0,1:T(2,128)S(1)}, f32[2048,2]{0,1:T(2,128)}, u32[]{:S(2)}) copy-start(f32[2048,2]{0,1:T(2,128)} %param.16) | copy-start | bytes 49156
  72.5 223.4 %all-gather.5.cloned.1.call-start = ((), (), s32[]{:S(2)}) async-start(), calls=%async_computation.5 | async-start | bytes 5849088 | tf_op jit(solution)/shard_map/all_gather | solution.py:97
  88.2 429.3 %all-reduce.6.cloned.1.call-start = ((), (), s32[]{:S(2)}) async-start(), calls=%async_computation.7 | async-start | bytes 11010048 | tf_op jit(solution)/shard_map/psum | solution.py:104
  290.8 2.9 copy-start.3
  295.9 3.6 copy-start.10
  308.5 216.5 %reduce-scatter.4.cloned.1.call-start = ((), (), s32[]{:S(2)}) async-start(), calls=%async_computation.6 | async-start | bytes 5849088
  308.9 7.0 %slice-start = ((s8[5505024]{0:T(1024)(128)(4,1)}), s8[1310720]{0:T(1024)(128)(4,1)S(1)}, s32[]{:S(2)}) async-start(s8[5505024]{0:T(1024)(128)(4,1)} %bitcast.64), calls=%async_computation.9 | async-start | bytes 2621440
  311.3 4.7 slice-start.1
  313.6 2.4 copy-start.2
  313.6 4.8 slice-start.4
  315.9 2.5 slice-start.5
  317.2 2.0 copy-start.4
  319.2 1.2 copy-start.12
  333.7 188.9 %slice-start.2 = ((s8[5505024]{0:T(1024)(128)(4,1)}), s8[1310720]{0:T(1024)(128)(4,1)S(1)}, s32[]{:S(2)}) async-start(s8[5505024]{0:T(1024)(128)(4,1)} %bitcast.66), calls=%async_computation.11 | async-start | bytes 2621440
  517.5 5.1 slice-start.3
  517.5 5.1 copy-start.11
  526.8 16.5 %all-to-all-start.2 = ((bf16[16,16,448]{2,1,0:T(8,128)(2,1)}), bf16[16,16,448]{2,1,0:T(8,128)(2,1)S(1)}, u32[]{:S(2)}, u32[]{:S(2)}) async-start(bf16[16,16,448]{2,1,0:T(8,128)(2,1)} %bitcast.14), calls=%async_computation.2 | async-start | bytes 524288 | tf_op jit(solution)/shard_map/all_to_all | solution.py:125
Sparse Core Ops, SparseCore 0:
  13.9 276.8 all-reduce.7
  308.6 208.8 all-reduce.5
Sparse Core Ops, SparseCore 1:
  72.6 76.9 all-gather.2
  151.1 79.8 all-gather.4
  333.8 76.0 reduce-scatter.3
where the time goes:
time: 553 us
  waiting for transfers between devices  389 us (70%)
  matrix products  42.6 us (8%)
  other arithmetic  41.9 us (8%)
  blocking collectives  32.7 us (6%)
  local copies, waits for them, and re-layouts  21.2 us (4%)
  between operations  16.9 us (3%)
  starting transfers between devices  8.03 us (1%)
    psum x1, waiting for transfers between devices, broadcast(): return lax.psum(block, axis)  202 us
    psum x1, waiting for transfers between devices, on_device(): lax.psum(hot_terms[0].astype(jnp.bfloat16), 'dp').astype(jnp.float32)  184 us
    another operation x1, other arithmetic, slot_tables(): before = jnp.cumsum(named_count, axis=1) - named_count  23.3 us
    all_to_all x1, blocking collectives, on_device(): lax.all_to_all(pack(tokens), 'dp', split_axis=0, concat_axis=0, tiled=True)  18 us
    all_to_all x1, blocking collectives, on_device(): lax.all_to_all(pack(grad_out), 'dp', split_axis=0, concat_axis=0, tiled=T...  14.7 us
    unnamed x43, local copies, waits for them, and re-layouts  11.1 us
  transfers between devices with their start and end apart: 6, of which 3 were waited for; matrix products, arithmetic and copies ran while one was open for 15% of the time, Pallas kernels for 0%

commit v1 on v0

--- a/solution.py
+++ b/solution.py
@@ -2,11 +2,6 @@
 import jax.numpy as jnp
 from jax import lax
 from jax.sharding import PartitionSpec as P
-
-
-def broadcast(block, axis, owner):
-    block = jnp.where(lax.axis_index(axis) == owner, block, jnp.zeros_like(block))
-    return lax.psum(block, axis)
 
 
 def slot_tables(routing, combine, hot_expert, dp_count, block_rows, expert_count, capacity):
@@ -29,16 +24,14 @@
     return (route_weight, slot_token, slot_live)
 
 
-def expert_terms(rows_in, rows_back, weight, gate_cols, up_cols, down_rows):
+def expert_terms(rows_in, rows_back, weight, gate_cols, up_cols, down_cols):
     across = (((1,), (1,)), ((), ()))
     downward = (((0,), (0,)), ((), ()))
     gate_pre = jnp.dot(rows_in, gate_cols, preferred_element_type=jnp.float32)
     up_pre = jnp.dot(rows_in, up_cols, preferred_element_type=jnp.float32)
     sigmoid_gate = jax.nn.sigmoid(gate_pre)
     active = gate_pre * sigmoid_gate
-    back_hidden = weight[:, None] * lax.dot_general(
-        rows_back, down_rows, across, preferred_element_type=jnp.float32
-    )
+    back_hidden = weight[:, None] * jnp.dot(rows_back, down_cols, preferred_element_type=jnp.float32)
     scaled = (weight[:, None] * active * up_pre).astype(jnp.bfloat16)
     grad_gate_pre = (
         back_hidden * up_pre * sigmoid_gate * (1.0 + gate_pre * (1.0 - sigmoid_gate))
@@ -46,7 +39,7 @@
     grad_up_pre = (back_hidden * active).astype(jnp.bfloat16)
     gate_sum = lax.dot_general(rows_in, grad_gate_pre, downward, preferred_element_type=jnp.float32)
     up_sum = lax.dot_general(rows_in, grad_up_pre, downward, preferred_element_type=jnp.float32)
-    down_sum = lax.dot_general(scaled, rows_back, downward, preferred_element_type=jnp.float32)
+    down_sum = lax.dot_general(rows_back, scaled, downward, preferred_element_type=jnp.float32)
     back = lax.dot_general(grad_gate_pre, gate_cols, across, preferred_element_type=jnp.float32)
     back = back + lax.dot_general(grad_up_pre, up_cols, across, preferred_element_type=jnp.float32)
     return (gate_sum, up_sum, down_sum, back)
@@ -56,8 +49,8 @@
     dp_count = lax.axis_size("dp")
     block_rows = tokens.shape[0]
     share_width = tokens.shape[1]
-    top_count = routing.shape[1]
-    capacity = block_rows * top_count // dp_count
+    width = w_gate.shape[1]
+    capacity = block_rows * routing.shape[1] // dp_count
     row_index = lax.axis_index("dp")
     hot_expert = hot_ids[0]
     route_weight, slot_token, slot_live = slot_tables(
@@ -74,11 +67,14 @@
     ).reshape(-1)
     block_weight = lax.dynamic_slice_in_dim(route_weight, row_index * block_rows, block_rows, 0)
     hot_weight = block_weight[:, hot_expert]
-    hot_gate_w, hot_up_w, hot_down_w = (
-        broadcast(w_gate[0], "dp", hot_expert),
-        broadcast(w_up[0], "dp", hot_expert),
-        broadcast(w_down[0], "dp", hot_expert),
-    )
+
+    own_down_cols = w_down[0].T
+    own = jnp.stack([w_gate[0], w_up[0], own_down_cols], 0)
+    own = own.reshape(3, dp_count, width // dp_count, own.shape[-1])
+    pieces = lax.all_to_all(own, "dp", split_axis=1, concat_axis=1, tiled=True)
+    hot_piece = lax.dynamic_index_in_dim(pieces, hot_expert, axis=1, keepdims=False)
+    hot_w = lax.all_gather(hot_piece, "dp", axis=1, tiled=True)
+    hot_gate_w, hot_up_w, hot_down_cols = hot_w[0], hot_w[1], hot_w[2]
 
     def pack(source):
         picked = jnp.take(source, send_token.reshape(-1), axis=0).reshape(
@@ -86,32 +82,32 @@
         )
         return jnp.where(send_live[:, :, None], picked, jnp.zeros_like(picked))
 
-    arrived_in, arrived_back = (
-        lax.all_to_all(pack(tokens), "dp", split_axis=0, concat_axis=0, tiled=True),
-        lax.all_to_all(pack(grad_out), "dp", split_axis=0, concat_axis=0, tiled=True),
+    packed = jnp.concatenate([pack(tokens), pack(grad_out)], 2)
+    arrived = lax.all_to_all(packed, "dp", split_axis=0, concat_axis=0, tiled=True)
+    arrived_in = arrived[:, :, :share_width].reshape(-1, share_width)
+    arrived_back = arrived[:, :, share_width:].reshape(-1, share_width)
+    local = jnp.stack(
+        [jnp.concatenate([tokens, arrived_in], 0), jnp.concatenate([grad_out, arrived_back], 0)], 0
     )
-    local_in = jnp.concatenate([tokens, arrived_in.reshape(-1, share_width)], 0)
-    local_back = jnp.concatenate([grad_out, arrived_back.reshape(-1, share_width)], 0)
-    full_in, full_back = (
-        lax.all_gather(local_in, "expert", axis=1, tiled=True),
-        lax.all_gather(local_back, "expert", axis=1, tiled=True),
-    )
+    full = lax.all_gather(local, "expert", axis=2, tiled=True)
+    full_in, full_back = full[0], full[1]
     hot_rows, cold_rows = (full_in[:block_rows], full_in[block_rows:])
     hot_cotan, cold_cotan = (full_back[:block_rows], full_back[block_rows:])
-    hot_terms = expert_terms(hot_rows, hot_cotan, hot_weight, hot_gate_w, hot_up_w, hot_down_w)
-    cold_terms = expert_terms(cold_rows, cold_cotan, cold_weight, w_gate[0], w_up[0], w_down[0])
-    summed = (
-        lax.psum(hot_terms[0].astype(jnp.bfloat16), "dp").astype(jnp.float32),
-        lax.psum(hot_terms[1].astype(jnp.bfloat16), "dp").astype(jnp.float32),
-        lax.psum(hot_terms[2].astype(jnp.bfloat16), "dp").astype(jnp.float32),
+    cold_terms = expert_terms(
+        cold_rows, cold_cotan, cold_weight, w_gate[0], w_up[0], own_down_cols
     )
+    hot_terms = expert_terms(hot_rows, hot_cotan, hot_weight, hot_gate_w, hot_up_w, hot_down_cols)
+
+    block_sums = jnp.stack([hot_terms[m].astype(jnp.bfloat16) for m in range(3)], 0)
+    block_sums = block_sums.reshape(3, dp_count, width // dp_count, block_sums.shape[-1])
+    by_chunk = lax.all_to_all(block_sums, "dp", split_axis=1, concat_axis=1, tiled=True)
+    chunk_sum = jnp.sum(by_chunk.astype(jnp.float32), axis=1).astype(jnp.bfloat16)
+    summed = lax.all_gather(chunk_sum, "dp", axis=1, tiled=True)
     owns_hot = row_index == hot_expert
-    expert_grads = tuple(
-        (
-            jnp.where(owns_hot, summed[member], cold_terms[member]).astype(jnp.bfloat16)[None]
-            for member in range(3)
-        )
-    )
+    grad_gate = jnp.where(owns_hot, summed[0], cold_terms[0].astype(jnp.bfloat16))
+    grad_up = jnp.where(owns_hot, summed[1], cold_terms[1].astype(jnp.bfloat16))
+    grad_down = jnp.where(owns_hot, summed[2], cold_terms[2].astype(jnp.bfloat16)).T
+
     positions = jnp.arange(block_rows, dtype=jnp.int32)
     select = (positions[:, None] == send_token.reshape(-1)[None, :]) & send_live.reshape(-1)[
         None, :
@@ -132,7 +128,7 @@
         preferred_element_type=jnp.float32,
     )
     token_grad = (hot_share + gathered_back).astype(jnp.bfloat16)
-    return (expert_grads[0], expert_grads[1], expert_grads[2], token_grad)
+    return (grad_gate[None], grad_up[None], grad_down[None], token_grad)
 
 
 def solution(mesh):

time: 553 us -> 575 us (1.040)
  waiting for transfers between devices: 389 us -> 223 us
  blocking collectives: 32.7 us -> 141 us
  local copies, waits for them, and re-layouts: 21.2 us -> 107 us
  matrix products: 42.6 us -> 32.4 us
    psum x2 -> x0, waiting for transfers between devices: 386 us -> none  [the longest x1 202 us: broadcast(): return lax.psum(block, axis)]
    all_to_all x0 -> x1, waiting for transfers between devices: none -> 171 us  [on_device(): pieces = lax.all_to_all(own, 'dp', split_axis=1, concat_axis=1, tiled=True)]
    all_to_all x2, blocking collectives: 32.7 us -> 141 us  [the longest x1 122 us: on_device(): lax.all_to_all(block_sums, 'dp', split_axis=1, concat_axis=1, tiled=True)]
    unnamed x43 -> x46, local copies, waits for them, and re-layouts: 11.1 us -> 70.6 us
    all_gather x2 -> x3, waiting for transfers between devices: 0.03 us -> 41.3 us  [the longest x1 41.3 us: on_device(): summed = lax.all_gather(chunk_sum, 'dp', axis=1, tiled=True)]
    slice x0 -> x3, local copies, waits for them, and re-layouts: none -> 24.3 us  [the longest x1 15.3 us: on_device(): hot_cotan, cold_cotan = (full_back[:block_rows], full_back[block_rows:])]
    all_to_all x1, waiting for transfers between devices: 3.57 us -> 10.8 us  [on_device(): lax.all_to_all(cold_share.astype(jnp.bfloat16), 'dp', split_axis=0, conca...]
  transfers between devices with their start and end apart: 6 -> 6, of which waited for: 3 -> 3; matrix products, arithmetic and copies ran while one was open for 15% -> 19% of each run, Pallas kernels for 0% -> 0%
where the time goes in v1:
time: 575 us; the launch traced here: 573 us
  waiting for transfers between devices  223 us (39%)
  blocking collectives  141 us (25%)
  local copies, waits for them, and re-layouts  107 us (19%)
  other arithmetic  45 us (8%)
  matrix products  32.4 us (6%)
  between operations  14.4 us (3%)
  starting transfers between devices  10.3 us (2%)
    all_to_all x1, waiting for transfers between devices, on_device(): pieces = lax.all_to_all(own, 'dp', split_axis=1, concat_axis=1, tiled=True)  171 us
    all_to_all x1, blocking collectives, on_device(): lax.all_to_all(block_sums, 'dp', split_axis=1, concat_axis=1, tiled=True)  122 us
    unnamed x46, local copies, waits for them, and re-layouts  70.6 us
    all_gather x1, waiting for transfers between devices, on_device(): summed = lax.all_gather(chunk_sum, 'dp', axis=1, tiled=True)  41.3 us
    another operation x1, other arithmetic, slot_tables(): before = jnp.cumsum(named_count, axis=1) - named_count  23.3 us
    all_to_all x1, blocking collectives, on_device(): lax.all_to_all(packed, 'dp', split_axis=0, concat_axis=0, tiled=True)  18.9 us
    slice x1, local copies, waits for them, and re-layouts, on_device(): hot_cotan, cold_cotan = (full_back[:block_rows], full_back[block_rows:])  15.3 us
  transfers between devices with their start and end apart: 6, of which 3 were waited for; matrix products, arithmetic and copies ran while one was open for 19% of the time, Pallas kernels for 0%

profile of v1, /device:TPU:1, one launch (start us, length us, event | category | flops | bytes accessed | tf_op | source)
XLA Modules:
  0.0 572.8 jit_solution(5800280438654190527)
XLA Ops:
  7.2 0.8 convert_reduce_fusion
  8.1 0.5 copy.97
  8.6 23.3 %fusion.63 = s32[16,128,16]{2,0,1:T(8,128)S(1)} fusion(s32[16,128,16]{2,0,1:T(8,128)S(1)} %copy.97), kind=kOutput, calls=%fused_computation.111 | output fusion | flops 4161536 | bytes 262144 | tf_op jit(solution)/shard_map/jit(cumsum)/reduce_window_sum | solution.py:14
  31.9 0.1 sub.13
  32.0 0.4 copy.99
  32.5 4.5 select_reduce_fusion
  37.1 4.6 fusion.34
  42.0 1.2 gather_fusion.1
  43.1 1.2 gather_fusion.2
  44.3 0.1 broadcast_select_fusion.1
  44.5 0.1 pad_maximum_fusion.4
  44.7 18.9 %all_to_all.20 = bf16[16,16,896]{2,1,0:T(8,128)(2,1)S(1)} all-to-all(bf16[16,16,896]{2,1,0:T(8,128)(2,1)S(1)} %pad_maximum_fusion.4), channel_id=1, replica_groups=mesh['dp'=16,'expert'=16] {'dp'}, dimensions={0} | all-to-all | bytes 917504 | tf_op jit(solution)/shard_map/all_to_all | solution.py:86
  63.6 0.1 fusion.62
  63.8 0.2 copy.105
  64.1 0.2 copy.103
  64.4 1.6 copy.106
  66.0 3.9 copy.109
  69.9 3.1 pad_maximum_fusion
  73.0 2.7 copy.110
  75.7 5.5 all-to-all-start.1
  81.4 170.8 %all-to-all-done.1 = bf16[3,16,448,128]{3,2,0,1:T(8,128)(2,1)} async-done(((bf16[3,16,448,128]{3,2,0,1:T(8,128)(2,1)}), bf16[3,16,448,128]{3,2,0,1:T(8,128)(2,1)}, u32[]{:S(2)}, u32[]{:S(2)}) %all-to-all-start.1) | async-done | bytes 5505056 | tf_op jit(solution)/shard_map/all_to_all | solution.py:74
  252.1 1.7 dynamic-slice_bitcast_fusion
  254.3 2.4 gather_fusion
  256.8 15.3 %fusion.61 = (bf16[1,256,7168]{1,0,2:T(2,128)(2,1)}, bf16[1,256,7168]{1,0,2:T(2,128)(2,1)}) fusion(bf16[2,384,7168]{1,0,2:T(2,128)(2,1)} %all-gather.5.cloned.1.call-done), kind=kLoop, calls=%fused_computation.109 | loop fusion | bytes 14680064 | tf_op jit(solution)/shard_map/slice | solution.py:95
  272.1 15.8 %copy.124 = bf16[1,256,7168]{2,1,0:T(8,128)(2,1)} copy(bf16[1,256,7168]{1,0,2:T(2,128)(2,1)} %get-tuple-element.32) | data formatting | bytes 7340032
  287.9 15.9 %copy.125 = bf16[1,256,7168]{2,1,0:T(8,128)(2,1)} copy(bf16[1,256,7168]{1,0,2:T(2,128)(2,1)} %get-tuple-element.31) | data formatting | bytes 7340032
  303.8 8.9 %fusion.60 = (bf16[1,128,7168]{1,0,2:T(2,128)(2,1)}, bf16[1,128,7168]{1,0,2:T(2,128)(2,1)}) fusion(bf16[2,384,7168]{1,0,2:T(2,128)(2,1)} %all-gather.5.cloned.1.call-done), kind=kLoop, calls=%fused_computation.108 | loop fusion | bytes 7340032 | tf_op jit(solution)/shard_map/slice | solution.py:94
  312.7 8.4 %copy.122 = bf16[1,128,7168]{2,1,0:T(8,128)(2,1)} copy(bf16[1,128,7168]{1,0,2:T(2,128)(2,1)} %get-tuple-element.30) | data formatting | bytes 3670016
  321.1 7.4 %copy.121 = bf16[1,128,7168]{2,1,0:T(8,128)(2,1)S(1)} copy(bf16[1,128,7168]{1,0,2:T(2,128)(2,1)} %get-tuple-element.29) | data formatting | bytes 3670016
  328.5 3.9 fusion.13
  332.4 0.4 copy-done.3
  332.7 1.2 fusion.15
  333.9 0.8 copy-done.8
  334.8 0.6 copy-done.10
  335.3 1.1 multiply_convert_fusion.1
  336.5 0.4 copy-done.4
  336.8 1.1 fusion.21
  337.9 3.0 fusion
  341.0 2.3 fusion.32
  343.3 2.5 fusion.42
  345.8 0.7 multiply_convert_fusion.6
  346.5 0.6 fusion.35
  347.1 0.7 fusion.1
  347.8 1.3 copy-done.5
  349.2 2.8 pad_maximum_fusion.2
  351.9 8.3 %copy.119 = bf16[384,7168]{0,1:T(8,128)(2,1)} copy(bf16[384,7168]{1,0:T(8,128)(2,1)} %pad_maximum_fusion.2) | data formatting | bytes 11010048
  360.3 0.7 convolution_convert_fusion.4
  361.0 0.7 convolution_convert_fusion.5
  361.7 0.8 copy-done.7
  362.5 0.7 convolution_convert_fusion.3
  363.2 0.9 pad_maximum_fusion.1
  364.1 122.3 %all_to_all.21 = bf16[3,16,448,128]{3,2,0,1:T(8,128)(2,1)} all-to-all(bf16[3,16,448,128]{3,2,0,1:T(8,128)(2,1)S(1)} %pad_maximum_fusion.1), channel_id=1, replica_groups=mesh['dp'=16,'expert'=16] {'dp'}, dimensions={1} | all-to-all | bytes 11010048 | tf_op jit(solution)/shard_map/all_to_all | solution.py:103
  486.4 4.3 reduce_sum.42
  490.7 1.0 slice.109
  491.6 0.8 copy.126
  492.5 4.7 all-to-all-start.3
  497.3 10.8 %all-to-all-done.3 = bf16[16,16,448]{2,1,0:T(8,128)(2,1)S(1)} async-done(((bf16[16,16,448]{2,1,0:T(8,128)(2,1)}), bf16[16,16,448]{2,1,0:T(8,128)(2,1)S(1)}, u32[]{:S(2)}, u32[]{:S(2)}) %all-to-all-start.3) | async-done | bytes 229408 | tf_op jit(solution)/shard_map/all_to_all | solution.py:121
  508.1 1.8 fusion.36
  509.9 41.3 %all-gather.7.cloned.1.call-done = bf16[3,7168,128]{2,1,0:T(8,128)(2,1)} async-done(((bf16[3,448,128]{2,1,0:T(8,128)(2,1)}), bf16[3,7168,128]{2,1,0:T(8,128)(2,1)}) %all-gather.7.cloned.1.call-update) | async-done | bytes 5505040 | tf_op jit(solution)/shard_map/all_gather | solution.py:105
  551.2 3.8 fusion.5
  555.0 2.9 copy.118
  557.9 5.2 fusion.7
  563.1 0.8 copy-done.16
  563.9 2.4 fusion.6
  (65 shorter events, 1.6 us)
Async XLA Ops:
  7.2 249.6 %all-gather.5.cloned.1.call-start = ((), (), s32[]{:S(2)}) async-start(), calls=%async_computation.5 | async-start | bytes 11698176 | tf_op jit(solution)/shard_map/all_gather | solution.py:92
  8.0 24.4 %copy-start.15 = (s32[16]{0:T(128)S(1)}, s32[16]{0:T(128)}, u32[]{:S(2)}) copy-start(s32[16]{0:T(128)} %param.17) | copy-start | bytes 196
  8.6 33.1 %copy-start.11 = (bf16[128,448]{0,1:T(8,128)(2,1)S(1)}, bf16[128,448]{0,1:T(8,128)(2,1)}, u32[]{:S(2)}) copy-start(bf16[128,448]{0,1:T(8,128)(2,1)} %param.10) | copy-start | bytes 344068
  8.6 33.3 %copy-start.12 = (bf16[128,448]{0,1:T(8,128)(2,1)S(1)}, bf16[128,448]{0,1:T(8,128)(2,1)}, u32[]{:S(2)}) copy-start(bf16[128,448]{0,1:T(8,128)(2,1)} %param.11) | copy-start | bytes 344068
  64.3 5.6 copy-start.2
  75.7 178.6 %copy-start.13 = (s32[2048,2]{0,1:T(2,128)S(1)}, s32[2048,2]{0,1:T(2,128)}, u32[]{:S(2)}) copy-start(s32[2048,2]{0,1:T(2,128)} %param.15) | copy-start | bytes 49156
  75.7 178.6 %copy-start.14 = (f32[2048,2]{0,1:T(2,128)S(1)}, f32[2048,2]{0,1:T(2,128)}, u32[]{:S(2)}) copy-start(f32[2048,2]{0,1:T(2,128)} %param.16) | copy-start | bytes 49156
  75.7 176.4 %all-to-all-start.1 = ((bf16[3,16,448,128]{3,2,0,1:T(8,128)(2,1)}), bf16[3,16,448,128]{3,2,0,1:T(8,128)(2,1)}, u32[]{:S(2)}, u32[]{:S(2)}) async-start(bf16[3,16,448,128]{3,2,0,1:T(8,128)(2,1)} %copy.110), calls=%async_computation.1 | async-start | bytes 11010048 | tf_op jit(solution)/shard_map/all_to_all | solution.py:74
  81.2 259.7 %all-gather.9.cloned.1.call-start = ((), (), s32[]{:S(2)}) async-start(), calls=%async_computation.7 | async-start | bytes 5849088 | tf_op jit(solution)/shard_map/all_gather | solution.py:76
  253.9 236.8 %reduce-scatter.4.cloned.1.call-start = ((), (), s32[]{:S(2)}) async-start(), calls=%async_computation.8 | async-start | bytes 5849088
  328.5 3.9 copy-start
  328.5 4.2 copy-start.3
  332.7 2.0 copy-start.8
  332.7 2.6 copy-start.10
  335.3 1.5 copy-start.4
  341.0 2.3 copy-start.6
  341.0 4.8 copy-start.9
  347.1 2.0 copy-start.5
  360.3 190.9 %all-gather.7.cloned.1.call-start = ((), (), s32[]{:S(2)}) async-start(), calls=%async_computation.6 | async-start | bytes 5849088 | tf_op jit(solution)/shard_map/all_gather | solution.py:105
  361.0 1.5 copy-start.7
  492.5 15.6 %all-to-all-start.3 = ((bf16[16,16,448]{2,1,0:T(8,128)(2,1)}), bf16[16,16,448]{2,1,0:T(8,128)(2,1)S(1)}, u32[]{:S(2)}, u32[]{:S(2)}) async-start(bf16[16,16,448]{2,1,0:T(8,128)(2,1)} %bitcast.37), calls=%async_computation.3 | async-start | bytes 524288 | tf_op jit(solution)/shard_map/all_to_all | solution.py:121
  557.9 5.2 copy-start.1
  557.9 6.0 %copy-start.16 = (bf16[3,7168,128]{2,1,0:T(8,128)(2,1)S(1)}, bf16[3,7168,128]{2,1,0:T(8,128)(2,1)}, u32[]{:S(2)}) copy-start(bf16[3,7168,128]{2,1,0:T(8,128)(2,1)} %all-gather.7.cloned.1.call-done) | copy-start | bytes 16515076
Sparse Core Ops, SparseCore 0:
  66.1 170.1 all-gather.4
  254.0 60.3 all-gather.8
  360.4 110.2 reduce-scatter.3
  490.8 60.3 all-gather.6

commit v2 on v1

--- a/solution.py
+++ b/solution.py
@@ -25,23 +25,23 @@
 
 
 def expert_terms(rows_in, rows_back, weight, gate_cols, up_cols, down_cols):
-    across = (((1,), (1,)), ((), ()))
-    downward = (((0,), (0,)), ((), ()))
-    gate_pre = jnp.dot(rows_in, gate_cols, preferred_element_type=jnp.float32)
-    up_pre = jnp.dot(rows_in, up_cols, preferred_element_type=jnp.float32)
+    gate_pre = jnp.einsum("srk,skh->rh", rows_in, gate_cols, preferred_element_type=jnp.float32)
+    up_pre = jnp.einsum("srk,skh->rh", rows_in, up_cols, preferred_element_type=jnp.float32)
     sigmoid_gate = jax.nn.sigmoid(gate_pre)
     active = gate_pre * sigmoid_gate
-    back_hidden = weight[:, None] * jnp.dot(rows_back, down_cols, preferred_element_type=jnp.float32)
+    back_hidden = weight[:, None] * jnp.einsum(
+        "srk,skh->rh", rows_back, down_cols, preferred_element_type=jnp.float32
+    )
     scaled = (weight[:, None] * active * up_pre).astype(jnp.bfloat16)
     grad_gate_pre = (
         back_hidden * up_pre * sigmoid_gate * (1.0 + gate_pre * (1.0 - sigmoid_gate))
     ).astype(jnp.bfloat16)
     grad_up_pre = (back_hidden * active).astype(jnp.bfloat16)
-    gate_sum = lax.dot_general(rows_in, grad_gate_pre, downward, preferred_element_type=jnp.float32)
-    up_sum = lax.dot_general(rows_in, grad_up_pre, downward, preferred_element_type=jnp.float32)
-    down_sum = lax.dot_general(rows_back, scaled, downward, preferred_element_type=jnp.float32)
-    back = lax.dot_general(grad_gate_pre, gate_cols, across, preferred_element_type=jnp.float32)
-    back = back + lax.dot_general(grad_up_pre, up_cols, across, preferred_element_type=jnp.float32)
+    gate_sum = jnp.einsum("srk,rh->skh", rows_in, grad_gate_pre, preferred_element_type=jnp.float32)
+    up_sum = jnp.einsum("srk,rh->skh", rows_in, grad_up_pre, preferred_element_type=jnp.float32)
+    down_sum = jnp.einsum("srk,rh->skh", rows_back, scaled, preferred_element_type=jnp.float32)
+    back = jnp.einsum("rh,skh->srk", grad_gate_pre, gate_cols, preferred_element_type=jnp.float32)
+    back = back + jnp.einsum("rh,skh->srk", grad_up_pre, up_cols, preferred_element_type=jnp.float32)
     return (gate_sum, up_sum, down_sum, back)
 
 
@@ -68,13 +68,12 @@
     block_weight = lax.dynamic_slice_in_dim(route_weight, row_index * block_rows, block_rows, 0)
     hot_weight = block_weight[:, hot_expert]
 
-    own_down_cols = w_down[0].T
-    own = jnp.stack([w_gate[0], w_up[0], own_down_cols], 0)
-    own = own.reshape(3, dp_count, width // dp_count, own.shape[-1])
+    share_count = lax.axis_size("expert")
+    own = jnp.stack([w_gate[0], w_up[0], w_down[0].T], 0)
+    own = own.reshape(3, share_count, width // share_count, own.shape[-1])
     pieces = lax.all_to_all(own, "dp", split_axis=1, concat_axis=1, tiled=True)
     hot_piece = lax.dynamic_index_in_dim(pieces, hot_expert, axis=1, keepdims=False)
-    hot_w = lax.all_gather(hot_piece, "dp", axis=1, tiled=True)
-    hot_gate_w, hot_up_w, hot_down_cols = hot_w[0], hot_w[1], hot_w[2]
+    hot_w = lax.all_gather(hot_piece, "dp", axis=1, tiled=True).reshape(own.shape)
 
     def pack(source):
         picked = jnp.take(source, send_token.reshape(-1), axis=0).reshape(
@@ -86,36 +85,30 @@
     arrived = lax.all_to_all(packed, "dp", split_axis=0, concat_axis=0, tiled=True)
     arrived_in = arrived[:, :, :share_width].reshape(-1, share_width)
     arrived_back = arrived[:, :, share_width:].reshape(-1, share_width)
-    local = jnp.stack(
-        [jnp.concatenate([tokens, arrived_in], 0), jnp.concatenate([grad_out, arrived_back], 0)], 0
-    )
-    full = lax.all_gather(local, "expert", axis=2, tiled=True)
-    full_in, full_back = full[0], full[1]
-    hot_rows, cold_rows = (full_in[:block_rows], full_in[block_rows:])
-    hot_cotan, cold_cotan = (full_back[:block_rows], full_back[block_rows:])
-    cold_terms = expert_terms(
-        cold_rows, cold_cotan, cold_weight, w_gate[0], w_up[0], own_down_cols
-    )
-    hot_terms = expert_terms(hot_rows, hot_cotan, hot_weight, hot_gate_w, hot_up_w, hot_down_cols)
+    full_in = lax.all_gather(jnp.concatenate([tokens, arrived_in], 0), "expert", axis=0)
+    full_back = lax.all_gather(jnp.concatenate([grad_out, arrived_back], 0), "expert", axis=0)
+    hot_rows, cold_rows = (full_in[:, :block_rows], full_in[:, block_rows:])
+    hot_cotan, cold_cotan = (full_back[:, :block_rows], full_back[:, block_rows:])
+    cold_terms = expert_terms(cold_rows, cold_cotan, cold_weight, own[0], own[1], own[2])
+    hot_terms = expert_terms(hot_rows, hot_cotan, hot_weight, hot_w[0], hot_w[1], hot_w[2])
 
     block_sums = jnp.stack([hot_terms[m].astype(jnp.bfloat16) for m in range(3)], 0)
-    block_sums = block_sums.reshape(3, dp_count, width // dp_count, block_sums.shape[-1])
     by_chunk = lax.all_to_all(block_sums, "dp", split_axis=1, concat_axis=1, tiled=True)
     chunk_sum = jnp.sum(by_chunk.astype(jnp.float32), axis=1).astype(jnp.bfloat16)
-    summed = lax.all_gather(chunk_sum, "dp", axis=1, tiled=True)
+    summed = lax.all_gather(chunk_sum, "dp", axis=1, tiled=True).reshape(block_sums.shape)
     owns_hot = row_index == hot_expert
-    grad_gate = jnp.where(owns_hot, summed[0], cold_terms[0].astype(jnp.bfloat16))
-    grad_up = jnp.where(owns_hot, summed[1], cold_terms[1].astype(jnp.bfloat16))
-    grad_down = jnp.where(owns_hot, summed[2], cold_terms[2].astype(jnp.bfloat16)).T
+    grads = jnp.where(owns_hot, summed, jnp.stack([cold_terms[m] for m in range(3)], 0))
+    grads = grads.astype(jnp.bfloat16).reshape(3, width, grads.shape[-1])
+    grad_gate, grad_up, grad_down = grads[0], grads[1], grads[2].T
 
     positions = jnp.arange(block_rows, dtype=jnp.int32)
     select = (positions[:, None] == send_token.reshape(-1)[None, :]) & send_live.reshape(-1)[
         None, :
     ]
-    stacked = jnp.concatenate([hot_terms[3], cold_terms[3]], 0)
+    stacked = jnp.concatenate([hot_terms[3], cold_terms[3]], 1)
     shares = lax.psum_scatter(
-        stacked.astype(jnp.bfloat16), "expert", scatter_dimension=1, tiled=True
-    ).astype(jnp.float32)
+        stacked.astype(jnp.bfloat16), "expert", scatter_dimension=0, tiled=True
+    )[0].astype(jnp.float32)
     hot_share = shares[:block_rows]
     cold_share = shares[block_rows:].reshape(dp_count, capacity, share_width)
     returned = lax.all_to_all(

time: 575 us -> 566 us (0.984)
  local copies, waits for them, and re-layouts: 107 us -> 27.1 us
  waiting for transfers between devices: 223 us -> 275 us
  matrix products: 32.4 us -> 44.8 us
  other arithmetic: 45 us -> 52 us
    all_gather x3 -> x4, waiting for transfers between devices: 41.3 us -> 148 us  [the longest x1 61.9 us: on_device(): lax.all_gather(hot_piece, 'dp', axis=1, tiled=True).reshape(own.shape)]
    unnamed x46 -> x22, local copies, waits for them, and re-layouts: 70.6 us -> 6.12 us
    all_to_all x1, waiting for transfers between devices: 171 us -> 122 us  [on_device(): pieces = lax.all_to_all(own, 'dp', split_axis=1, concat_axis=1, tiled=True)]
    slice x2, local copies, waits for them, and re-layouts: 24.1 us -> 5.15 us  [the longest x1 2.96 us: on_device(): hot_w[2]]
    dot_general x16, matrix products: 30.5 us -> 43 us  [the longest x2 7.23 us: expert_terms(): jnp.einsum('srk,rh->skh', rows_back, scaled, preferred_element_type=jnp.f...]
    all_to_all x1, waiting for transfers between devices: 10.8 us -> 4.2 us  [on_device(): lax.all_to_all(cold_share.astype(jnp.bfloat16), 'dp', split_axis=0, conca...]
  transfers between devices with their start and end apart: 6 -> 7, of which waited for: 3 -> 5; matrix products, arithmetic and copies ran while one was open for 19% -> 10% of each run, Pallas kernels for 0% -> 0%
where the time goes in v2:
time: 566 us; the launch traced here: 565 us
  waiting for transfers between devices  275 us (49%)
  blocking collectives  141 us (25%)
  other arithmetic  52 us (9%)
  matrix products  44.8 us (8%)
  local copies, waits for them, and re-layouts  27.1 us (5%)
  between operations  14.3 us (3%)
  starting transfers between devices  10.8 us (2%)
    all_to_all x1, waiting for transfers between devices, on_device(): pieces = lax.all_to_all(own, 'dp', split_axis=1, concat_axis=1, tiled=True)  122 us
    all_to_all x1, blocking collectives, on_device(): lax.all_to_all(block_sums, 'dp', split_axis=1, concat_axis=1, tiled=True)  122 us
    all_gather x1, waiting for transfers between devices, on_device(): lax.all_gather(hot_piece, 'dp', axis=1, tiled=True).reshape(own.shape)  61.9 us
    all_gather x1, waiting for transfers between devices, on_device(): lax.all_gather(jnp.concatenate([grad_out, arrived_back], 0), 'expert', ax...  51.6 us
    all_gather x1, waiting for transfers between devices, on_device(): lax.all_gather(chunk_sum, 'dp', axis=1, tiled=True)  34.6 us
    another operation x1, other arithmetic, slot_tables(): before = jnp.cumsum(named_count, axis=1) - named_count  23.3 us
    all_to_all x1, blocking collectives, on_device(): lax.all_to_all(packed, 'dp', split_axis=0, concat_axis=0, tiled=True)  18.9 us
  transfers between devices with their start and end apart: 7, of which 5 were waited for; matrix products, arithmetic and copies ran while one was open for 10% of the time, Pallas kernels for 0%

profile of v2, /device:TPU:1, one launch (start us, length us, event | category | flops | bytes accessed | tf_op | source)
XLA Modules:
  0.0 564.6 jit_solution(10148111566144932478)
XLA Ops:
  7.2 0.8 convert_reduce_fusion
  8.1 0.5 copy.81
  8.6 23.3 %fusion.98 = s32[16,128,16]{2,0,1:T(8,128)S(1)} fusion(s32[16,128,16]{2,0,1:T(8,128)S(1)} %copy.81), kind=kOutput, calls=%fused_computation.114 | output fusion | flops 4161536 | bytes 262144 | tf_op jit(solution)/shard_map/jit(cumsum)/reduce_window_sum | solution.py:14
  31.9 0.1 sub.13
  32.0 0.4 copy.83
  32.5 4.5 select_reduce_fusion
  37.1 4.6 fusion.31
  41.7 0.1 copy.85
  41.9 0.1 copy.86
  42.0 1.2 gather_fusion.2
  43.1 1.2 gather_fusion.1
  44.3 0.1 broadcast_select_fusion.1
  44.4 0.1 broadcast_select_fusion.3
  44.5 0.1 pad_maximum_fusion.3
  44.7 18.9 %all_to_all.20 = bf16[16,16,896]{2,1,0:T(8,128)(2,1)S(1)} all-to-all(bf16[16,16,896]{2,1,0:T(8,128)(2,1)S(1)} %pad_maximum_fusion.3), channel_id=1, replica_groups=mesh['dp'=16,'expert'=16] {'dp'}, dimensions={0} | all-to-all | bytes 917504 | tf_op jit(solution)/shard_map/all_to_all | solution.py:85
  63.6 0.1 fusion.93
  63.7 0.8 pad_maximum_fusion.4
  64.6 0.8 pad_maximum_fusion.5
  65.4 3.9 copy.92
  69.3 3.1 pad_maximum_fusion
  72.4 2.8 copy.93
  75.2 5.5 all-to-all-start.1
  80.9 122.4 %all-to-all-done.1 = bf16[3,16,448,128]{3,2,0,1:T(8,128)(2,1)} async-done(((bf16[3,16,448,128]{3,2,0,1:T(8,128)(2,1)}), bf16[3,16,448,128]{3,2,0,1:T(8,128)(2,1)}, u32[]{:S(2)}, u32[]{:S(2)}) %all-to-all-start.1) | async-done | bytes 5505056 | tf_op jit(solution)/shard_map/all_to_all | solution.py:74
  203.3 1.7 constant_dynamic-slice_fusion.1
  205.1 0.2 reduce-scatter.2.cloned.1.call-start
  205.6 0.1 squeeze.44
  205.7 2.4 gather_fusion
  208.2 3.6 fusion.40
  211.8 0.6 copy-done
  212.3 2.7 fusion.43
  215.0 51.6 %all-gather.12.cloned.1.call-done = bf16[6144,448]{1,0:T(8,128)(2,1)} async-done(((bf16[384,448]{1,0:T(8,128)(2,1)}), bf16[6144,448]{1,0:T(8,128)(2,1)}) %all-gather.12.cloned.1.call-update) | async-done | bytes 5505040 | tf_op jit(solution)/shard_map/all_gather | solution.py:89
  266.6 4.0 multiply_convert_fusion.2
  270.6 1.1 fusion.70
  271.7 3.0 fusion.5
  274.7 61.9 %all-gather.14.cloned.1.call-done = bf16[3,1,7168,128]{3,2,0,1:T(8,128)(2,1)} async-done(((bf16[3,1,448,128]{3,2,0,1:T(8,128)(2,1)}), bf16[3,1,7168,128]{3,2,0,1:T(8,128)(2,1)}) %all-gather.14.cloned.1.call-update) | async-done | bytes 5505040 | tf_op jit(solution)/shard_map/all_gather | solution.py:76
  336.7 3.0 fusion.92
  339.6 2.3 fusion.52
  342.0 2.3 fusion.55
  344.3 2.3 multiply_convert_fusion.5
  346.7 0.6 fusion.80
  347.3 0.6 fusion.32
  347.9 1.4 copy-done.1
  349.3 3.2 pad_maximum_fusion.2
  352.6 0.3 all-gather.8.cloned.1.call-start
  352.9 2.3 convert_bitcast_fusion.2
  355.2 2.3 convert_bitcast_fusion.1
  357.5 2.4 convert_bitcast_fusion
  359.9 0.9 pad_maximum_fusion.1
  360.8 0.4 copy.94
  361.2 121.9 %all_to_all.21 = bf16[3,16,448,128]{3,2,0,1:T(8,128)(2,1)} all-to-all(bf16[3,16,448,128]{3,2,0,1:T(8,128)(2,1)S(1)} %copy.94), channel_id=1, replica_groups=mesh['dp'=16,'expert'=16] {'dp'}, dimensions={1} | all-to-all | bytes 11010048 | tf_op jit(solution)/shard_map/all_to_all | solution.py:96
  483.1 4.3 reduce_sum.42
  487.4 0.1 and.35
  487.5 3.6 fusion.19
  491.1 4.9 fusion.22
  496.0 1.0 slice.111
  496.9 0.8 copy.98
  497.8 4.7 all-to-all-start.3
  502.5 4.8 fusion.16
  507.3 4.2 all-to-all-done.3
  511.5 1.8 fusion.39
  513.3 34.6 %all-gather.8.cloned.1.call-done = bf16[3,7168,128]{2,1,0:T(8,128)(2,1)} async-done(((bf16[3,448,128]{2,1,0:T(8,128)(2,1)}), bf16[3,7168,128]{2,1,0:T(8,128)(2,1)}) %all-gather.8.cloned.1.call-update) | async-done | bytes 5505040 | tf_op jit(solution)/shard_map/all_gather | solution.py:98
  547.9 5.1 fusion
  553.0 2.2 fusion.91
  555.2 2.9 copy.97
  (45 shorter events, 0.8 us)
Async XLA Ops:
  7.2 201.0 %all-gather.10.cloned.1.call-start = ((), (), s32[]{:S(2)}) async-start(), calls=%async_computation.7 | async-start | bytes 6684672 | tf_op jit(solution)/shard_map/all_gather | solution.py:88
  8.0 24.4 %copy-start.8 = (s32[16]{0:T(128)S(1)}, s32[16]{0:T(128)}, u32[]{:S(2)}) copy-start(s32[16]{0:T(128)} %param.17) | copy-start | bytes 196
  8.6 33.1 %copy-start.4 = (bf16[128,448]{0,1:T(8,128)(2,1)S(1)}, bf16[128,448]{0,1:T(8,128)(2,1)}, u32[]{:S(2)}) copy-start(bf16[128,448]{0,1:T(8,128)(2,1)} %param.11) | copy-start | bytes 344068
  8.6 33.3 %copy-start.5 = (bf16[128,448]{0,1:T(8,128)(2,1)S(1)}, bf16[128,448]{0,1:T(8,128)(2,1)}, u32[]{:S(2)}) copy-start(bf16[128,448]{0,1:T(8,128)(2,1)} %param.10) | copy-start | bytes 344068
  63.6 5.7 %copy-start.2 = (bf16[1,7168,128]{2,1,0:T(8,128)(2,1)S(1)}, bf16[1,7168,128]{2,1,0:T(8,128)(2,1)}, u32[]{:S(2)}) copy-start(bf16[1,7168,128]{2,1,0:T(8,128)(2,1)} %param.13) | copy-start | bytes 5505028
  64.5 202.0 %all-gather.12.cloned.1.call-start = ((), (), s32[]{:S(2)}) async-start(), calls=%async_computation.8 | async-start | bytes 6684672 | tf_op jit(solution)/shard_map/all_gather | solution.py:89
  75.2 130.5 %copy-start.6 = (s32[2048,2]{0,1:T(2,128)S(1)}, s32[2048,2]{0,1:T(2,128)}, u32[]{:S(2)}) copy-start(s32[2048,2]{0,1:T(2,128)} %param.15) | copy-start | bytes 49156
  75.2 130.5 %copy-start.7 = (f32[2048,2]{0,1:T(2,128)S(1)}, f32[2048,2]{0,1:T(2,128)}, u32[]{:S(2)}) copy-start(f32[2048,2]{0,1:T(2,128)} %param.16) | copy-start | bytes 49156
  75.2 128.1 %all-to-all-start.1 = ((bf16[3,16,448,128]{3,2,0,1:T(8,128)(2,1)}), bf16[3,16,448,128]{3,2,0,1:T(8,128)(2,1)}, u32[]{:S(2)}, u32[]{:S(2)}) async-start(bf16[3,16,448,128]{3,2,0,1:T(8,128)(2,1)} %copy.93), calls=%async_computation.1 | async-start | bytes 11010048 | tf_op jit(solution)/shard_map/all_to_all | solution.py:74
  80.7 255.9 %all-gather.14.cloned.1.call-start = ((), (), s32[]{:S(2)}) async-start(), calls=%async_computation.9 | async-start | bytes 5849088 | tf_op jit(solution)/shard_map/all_gather | solution.py:76
  205.1 290.9 %reduce-scatter.2.cloned.1.call-start = ((), (), s32[]{:S(2)}) async-start(), calls=%async_computation.6 | async-start | bytes 5849088 | tf_op jit(solution)/shard_map/reduce_scatter | solution.py:109
  208.2 4.1 copy-start
  266.6 4.1 copy-start.3
  347.3 2.0 copy-start.1
  352.6 195.3 %all-gather.8.cloned.1.call-start = ((), (), s32[]{:S(2)}) async-start(), calls=%async_computation.5 | async-start | bytes 5849088 | tf_op jit(solution)/shard_map/all_gather | solution.py:98
  497.8 13.8 %all-to-all-start.3 = ((bf16[16,16,448]{2,1,0:T(8,128)(2,1)}), bf16[16,16,448]{2,1,0:T(8,128)(2,1)S(1)}, u32[]{:S(2)}, u32[]{:S(2)}) async-start(bf16[16,16,448]{2,1,0:T(8,128)(2,1)} %bitcast.49), calls=%async_computation.4 | async-start | bytes 524288 | tf_op jit(solution)/shard_map/all_to_all | solution.py:114
Sparse Core Ops, SparseCore 0:
  64.7 111.2 all-gather.9
  178.3 88.1 all-gather.11
  269.3 67.3 all-gather.13
  352.7 115.1 reduce-scatter.1
  487.5 60.3 all-gather.7

commit v3 on v2

--- a/solution.py
+++ b/solution.py
@@ -11,14 +11,17 @@
     named_count = jnp.sum(name_match.astype(jnp.int32), axis=1).reshape(
         dp_count, block_rows, expert_count
     )
-    before = jnp.cumsum(named_count, axis=1) - named_count
+    positions = jnp.arange(block_rows, dtype=jnp.int32)
+    earlier = (positions[None, :] < positions[:, None]).astype(jnp.bfloat16)
+    before = jnp.einsum(
+        "ts,bse->bte", earlier, named_count.astype(jnp.bfloat16), preferred_element_type=jnp.float32
+    ).astype(jnp.int32)
     slot_ids = jnp.arange(capacity, dtype=jnp.int32)
     slot_match = (
         (named_count[..., None] == 1)
         & (before[..., None] == slot_ids)
         & (columns != hot_expert)[None, None, :, None]
     )
-    positions = jnp.arange(block_rows, dtype=jnp.int32)
     slot_token = jnp.sum(jnp.where(slot_match, positions[None, :, None, None], 0), axis=1)
     slot_live = jnp.any(slot_match, axis=1)
     return (route_weight, slot_token, slot_live)

time: 566 us -> 544 us (0.961)
  other arithmetic: 52 us -> 29.1 us
    another operation x1 -> x0, other arithmetic: 23.3 us -> none  [slot_tables(): before = jnp.cumsum(named_count, axis=1) - named_count]
  transfers between devices with their start and end apart: 7 -> 7, of which waited for: 5 -> 5; matrix products, arithmetic and copies ran while one was open for 10% -> 11% of each run, Pallas kernels for 0% -> 0%
where the time goes in v3:
time: 544 us; the launch traced here: 543 us
  waiting for transfers between devices  275 us (51%)
  blocking collectives  141 us (26%)
  matrix products  45 us (8%)
  other arithmetic  29.1 us (5%)
  local copies, waits for them, and re-layouts  27.9 us (5%)
  between operations  14.3 us (3%)
  starting transfers between devices  10.8 us (2%)
    all_to_all x1, waiting for transfers between devices, on_device(): pieces = lax.all_to_all(own, 'dp', split_axis=1, concat_axis=1, tiled=True)  122 us
    all_to_all x1, blocking collectives, on_device(): lax.all_to_all(block_sums, 'dp', split_axis=1, concat_axis=1, tiled=True)  122 us
    all_gather x1, waiting for transfers between devices, on_device(): lax.all_gather(hot_piece, 'dp', axis=1, tiled=True).reshape(own.shape)  62 us
    all_gather x1, waiting for transfers between devices, on_device(): lax.all_gather(jnp.concatenate([grad_out, arrived_back], 0), 'expert', ax...  51.5 us
    all_gather x1, waiting for transfers between devices, on_device(): lax.all_gather(chunk_sum, 'dp', axis=1, tiled=True)  34.6 us
    all_to_all x1, blocking collectives, on_device(): lax.all_to_all(packed, 'dp', split_axis=0, concat_axis=0, tiled=True)  18.9 us
  transfers between devices with their start and end apart: 7, of which 5 were waited for; matrix products, arithmetic and copies ran while one was open for 11% of the time, Pallas kernels for 0%

profile of v3, /device:TPU:1, one launch (start us, length us, event | category | flops | bytes accessed | tf_op | source)
XLA Modules:
  0.0 542.7 jit_solution(13867141984875255845)
XLA Ops:
  7.2 0.8 convert_reduce_fusion
  8.0 0.2 fusion.49
  8.2 0.7 iota_compare_fusion.4
  8.8 4.5 select_reduce_fusion
  13.5 4.6 fusion.31
  18.0 1.0 copy.79
  19.0 1.0 copy.80
  20.0 1.2 gather_fusion.2
  21.2 1.2 gather_fusion.1
  22.4 0.1 broadcast_select_fusion.1
  22.5 0.1 broadcast_select_fusion.3
  22.6 0.1 pad_maximum_fusion.3
  22.7 18.9 %all_to_all.20 = bf16[16,16,896]{2,1,0:T(8,128)(2,1)S(1)} all-to-all(bf16[16,16,896]{2,1,0:T(8,128)(2,1)S(1)} %pad_maximum_fusion.3), channel_id=1, replica_groups=mesh['dp'=16,'expert'=16] {'dp'}, dimensions={0} | all-to-all | bytes 917504 | tf_op jit(solution)/shard_map/all_to_all | solution.py:88
  41.7 0.1 fusion.98
  41.8 0.8 pad_maximum_fusion.4
  42.7 0.8 pad_maximum_fusion.5
  43.5 3.9 copy.86
  47.4 3.1 pad_maximum_fusion
  50.5 2.8 copy.87
  53.3 5.5 %all-to-all-start.1 = ((bf16[3,16,448,128]{3,2,0,1:T(8,128)(2,1)}), bf16[3,16,448,128]{3,2,0,1:T(8,128)(2,1)}, u32[]{:S(2)}, u32[]{:S(2)}) async-start(bf16[3,16,448,128]{3,2,0,1:T(8,128)(2,1)} %copy.87), calls=%async_computation.1 | async-start | bytes 11010048 | tf_op jit(solution)/shard_map/all_to_all | solution.py:77
  59.0 122.4 %all-to-all-done.1 = bf16[3,16,448,128]{3,2,0,1:T(8,128)(2,1)} async-done(((bf16[3,16,448,128]{3,2,0,1:T(8,128)(2,1)}), bf16[3,16,448,128]{3,2,0,1:T(8,128)(2,1)}, u32[]{:S(2)}, u32[]{:S(2)}) %all-to-all-start.1) | async-done | bytes 5505056 | tf_op jit(solution)/shard_map/all_to_all | solution.py:77
  181.4 1.7 constant_dynamic-slice_fusion.1
  183.2 0.2 reduce-scatter.2.cloned.1.call-start
  183.5 0.1 reshape.160
  183.6 0.1 squeeze.44
  183.8 2.4 gather_fusion
  186.2 0.1 dynamic-slice_bitcast_fusion
  186.2 3.6 fusion.40
  189.8 0.6 copy-done
  190.4 2.7 fusion.43
  193.1 51.5 %all-gather.12.cloned.1.call-done = bf16[6144,448]{1,0:T(8,128)(2,1)} async-done(((bf16[384,448]{1,0:T(8,128)(2,1)}), bf16[6144,448]{1,0:T(8,128)(2,1)}) %all-gather.12.cloned.1.call-update) | async-done | bytes 5505040 | tf_op jit(solution)/shard_map/all_gather | solution.py:92
  244.6 4.0 multiply_convert_fusion.2
  248.7 1.1 fusion.73
  249.8 3.0 fusion.5
  252.8 62.0 %all-gather.14.cloned.1.call-done = bf16[3,1,7168,128]{3,2,0,1:T(8,128)(2,1)} async-done(((bf16[3,1,448,128]{3,2,0,1:T(8,128)(2,1)}), bf16[3,1,7168,128]{3,2,0,1:T(8,128)(2,1)}) %all-gather.14.cloned.1.call-update) | async-done | bytes 5505040 | tf_op jit(solution)/shard_map/all_gather | solution.py:79
  314.8 3.0 fusion.97
  317.7 2.3 fusion.53
  320.1 2.3 fusion.56
  322.4 2.3 multiply_convert_fusion.5
  324.8 0.6 fusion.85
  325.4 0.6 fusion.32
  326.1 1.4 copy-done.1
  327.4 3.3 pad_maximum_fusion.2
  330.7 0.3 all-gather.8.cloned.1.call-start
  331.0 2.3 convert_bitcast_fusion.2
  333.3 2.3 convert_bitcast_fusion.1
  335.7 2.4 convert_bitcast_fusion
  338.0 0.9 pad_maximum_fusion.1
  339.0 0.4 copy.88
  339.3 121.9 %all_to_all.21 = bf16[3,16,448,128]{3,2,0,1:T(8,128)(2,1)} all-to-all(bf16[3,16,448,128]{3,2,0,1:T(8,128)(2,1)S(1)} %copy.88), channel_id=1, replica_groups=mesh['dp'=16,'expert'=16] {'dp'}, dimensions={1} | all-to-all | bytes 11010048 | tf_op jit(solution)/shard_map/all_to_all | solution.py:99
  461.2 4.3 reduce_sum.42
  465.5 0.1 and.35
  465.6 3.6 fusion.19
  469.2 4.9 fusion.22
  474.1 1.0 slice.111
  475.1 0.8 copy.92
  475.9 4.7 all-to-all-start.3
  480.6 4.8 fusion.16
  485.4 4.2 all-to-all-done.3
  489.6 1.8 fusion.39
  491.5 34.6 %all-gather.8.cloned.1.call-done = bf16[3,7168,128]{2,1,0:T(8,128)(2,1)} async-done(((bf16[3,448,128]{2,1,0:T(8,128)(2,1)}), bf16[3,7168,128]{2,1,0:T(8,128)(2,1)}) %all-gather.8.cloned.1.call-update) | async-done | bytes 5505040 | tf_op jit(solution)/shard_map/all_gather | solution.py:101
  526.0 5.1 fusion
  531.1 2.2 fusion.96
  533.3 2.9 copy.91
  (36 shorter events, 0.5 us)
Async XLA Ops:
  7.2 179.1 %all-gather.10.cloned.1.call-start = ((), (), s32[]{:S(2)}) async-start(), calls=%async_computation.7 | async-start | bytes 6684672 | tf_op jit(solution)/shard_map/all_gather | solution.py:91
  41.7 5.7 %copy-start.2 = (bf16[1,7168,128]{2,1,0:T(8,128)(2,1)S(1)}, bf16[1,7168,128]{2,1,0:T(8,128)(2,1)}, u32[]{:S(2)}) copy-start(bf16[1,7168,128]{2,1,0:T(8,128)(2,1)} %param.13) | copy-start | bytes 5505028
  42.6 202.0 %all-gather.12.cloned.1.call-start = ((), (), s32[]{:S(2)}) async-start(), calls=%async_computation.8 | async-start | bytes 6684672 | tf_op jit(solution)/shard_map/all_gather | solution.py:92
  53.3 5.6 %copy-start.6 = (s32[16]{0:T(128)S(1)}, s32[16]{0:T(128)}, u32[]{:S(2)}) copy-start(s32[16]{0:T(128)} %param.17) | copy-start | bytes 196
  53.3 130.5 %copy-start.4 = (s32[2048,2]{0,1:T(2,128)S(1)}, s32[2048,2]{0,1:T(2,128)}, u32[]{:S(2)}) copy-start(s32[2048,2]{0,1:T(2,128)} %param.15) | copy-start | bytes 49156
  53.3 130.5 %copy-start.5 = (f32[2048,2]{0,1:T(2,128)S(1)}, f32[2048,2]{0,1:T(2,128)}, u32[]{:S(2)}) copy-start(f32[2048,2]{0,1:T(2,128)} %param.16) | copy-start | bytes 49156
  53.3 128.1 %all-to-all-start.1 = ((bf16[3,16,448,128]{3,2,0,1:T(8,128)(2,1)}), bf16[3,16,448,128]{3,2,0,1:T(8,128)(2,1)}, u32[]{:S(2)}, u32[]{:S(2)}) async-start(bf16[3,16,448,128]{3,2,0,1:T(8,128)(2,1)} %copy.87), calls=%async_computation.1 | async-start | bytes 11010048 | tf_op jit(solution)/shard_map/all_to_all | solution.py:77
  58.8 256.0 %all-gather.14.cloned.1.call-start = ((), (), s32[]{:S(2)}) async-start(), calls=%async_computation.9 | async-start | bytes 5849088 | tf_op jit(solution)/shard_map/all_gather | solution.py:79
  183.2 290.9 %reduce-scatter.2.cloned.1.call-start = ((), (), s32[]{:S(2)}) async-start(), calls=%async_computation.6 | async-start | bytes 5849088 | tf_op jit(solution)/shard_map/reduce_scatter | solution.py:112
  186.2 4.1 copy-start
  244.6 4.1 copy-start.3
  325.4 2.0 copy-start.1
  330.7 195.3 %all-gather.8.cloned.1.call-start = ((), (), s32[]{:S(2)}) async-start(), calls=%async_computation.5 | async-start | bytes 5849088 | tf_op jit(solution)/shard_map/all_gather | solution.py:101
  475.9 13.7 %all-to-all-start.3 = ((bf16[16,16,448]{2,1,0:T(8,128)(2,1)}), bf16[16,16,448]{2,1,0:T(8,128)(2,1)S(1)}, u32[]{:S(2)}, u32[]{:S(2)}) async-start(bf16[16,16,448]{2,1,0:T(8,128)(2,1)} %bitcast.51), calls=%async_computation.4 | async-start | bytes 524288 | tf_op jit(solution)/shard_map/all_to_all | solution.py:117
Sparse Core Ops, SparseCore 0:
  42.7 111.2 all-gather.9
  156.4 88.1 all-gather.11
  247.4 67.3 all-gather.13
  330.8 115.2 reduce-scatter.1
  465.6 60.3 all-gather.7

commit v4 on v3

--- a/solution.py
+++ b/solution.py
@@ -88,8 +88,11 @@
     arrived = lax.all_to_all(packed, "dp", split_axis=0, concat_axis=0, tiled=True)
     arrived_in = arrived[:, :, :share_width].reshape(-1, share_width)
     arrived_back = arrived[:, :, share_width:].reshape(-1, share_width)
-    full_in = lax.all_gather(jnp.concatenate([tokens, arrived_in], 0), "expert", axis=0)
-    full_back = lax.all_gather(jnp.concatenate([grad_out, arrived_back], 0), "expert", axis=0)
+    local = jnp.stack(
+        [jnp.concatenate([tokens, arrived_in], 0), jnp.concatenate([grad_out, arrived_back], 0)], 0
+    )
+    full = lax.all_gather(local, "expert", axis=1)
+    full_in, full_back = full[0], full[1]
     hot_rows, cold_rows = (full_in[:, :block_rows], full_in[:, block_rows:])
     hot_cotan, cold_cotan = (full_back[:, :block_rows], full_back[:, block_rows:])
     cold_terms = expert_terms(cold_rows, cold_cotan, cold_weight, own[0], own[1], own[2])

time: 544 us -> 561 us (1.031)
  waiting for transfers between devices: 275 us -> 291 us
  matrix products: 45 us -> 31.6 us
  local copies, waits for them, and re-layouts: 27.9 us -> 35.8 us
    all_gather x2 -> x1, waiting for transfers between devices: 51.5 us -> 138 us  [on_device(): full = lax.all_gather(local, 'expert', axis=1)]
    all_to_all x1, waiting for transfers between devices: 122 us -> 79.6 us  [on_device(): pieces = lax.all_to_all(own, 'dp', split_axis=1, concat_axis=1, tiled=True)]
    all_gather x1, waiting for transfers between devices: 62 us -> 34.6 us  [on_device(): lax.all_gather(hot_piece, 'dp', axis=1, tiled=True).reshape(own.shape)]
    all_to_all x1, blocking collectives: 18.9 us -> 24.5 us  [on_device(): lax.all_to_all(packed, 'dp', split_axis=0, concat_axis=0, tiled=True)]
  transfers between devices with their start and end apart: 7 -> 6, of which waited for: 5 -> 5; matrix products, arithmetic and copies ran while one was open for 11% -> 9% of each run, Pallas kernels for 0% -> 0%
where the time goes in v4:
time: 561 us; the launch traced here: 560 us
  waiting for transfers between devices  291 us (52%)
  blocking collectives  146 us (26%)
  local copies, waits for them, and re-layouts  35.8 us (6%)
  matrix products  31.6 us (6%)
  other arithmetic  27.3 us (5%)
  between operations  14.3 us (3%)
  starting transfers between devices  13.8 us (2%)
    all_gather x1, waiting for transfers between devices, on_device(): full = lax.all_gather(local, 'expert', axis=1)  138 us
    all_to_all x1, blocking collectives, on_device(): lax.all_to_all(block_sums, 'dp', split_axis=1, concat_axis=1, tiled=True)  121 us
    all_to_all x1, waiting for transfers between devices, on_device(): pieces = lax.all_to_all(own, 'dp', split_axis=1, concat_axis=1, tiled=True)  79.6 us
    all_gather x1, waiting for transfers between devices, on_device(): lax.all_gather(chunk_sum, 'dp', axis=1, tiled=True)  34.8 us
    all_gather x1, waiting for transfers between devices, on_device(): lax.all_gather(hot_piece, 'dp', axis=1, tiled=True).reshape(own.shape)  34.6 us
    all_to_all x1, blocking collectives, on_device(): lax.all_to_all(packed, 'dp', split_axis=0, concat_axis=0, tiled=True)  24.5 us
  transfers between devices with their start and end apart: 6, of which 5 were waited for; matrix products, arithmetic and copies ran while one was open for 9% of the time, Pallas kernels for 0%

profile of v4, /device:TPU:1, one launch (start us, length us, event | category | flops | bytes accessed | tf_op | source)
XLA Modules:
  0.0 559.9 jit_solution(10683196931715748003)
XLA Ops:
  7.2 4.0 copy.86
  11.2 3.1 pad_maximum_fusion
  14.3 2.8 copy.87
  17.1 8.6 %all-to-all-start.1 = ((bf16[3,16,448,128]{3,2,0,1:T(8,128)(2,1)}), bf16[3,16,448,128]{3,2,0,1:T(8,128)(2,1)}, u32[]{:S(2)}, u32[]{:S(2)}) async-start(bf16[3,16,448,128]{3,2,0,1:T(8,128)(2,1)} %copy.87), calls=%async_computation.1 | async-start | bytes 11010048 | tf_op jit(solution)/shard_map/all_to_all | solution.py:77
  25.9 79.6 %all-to-all-done.1 = bf16[3,16,448,128]{3,2,0,1:T(8,128)(2,1)} async-done(((bf16[3,16,448,128]{3,2,0,1:T(8,128)(2,1)}), bf16[3,16,448,128]{3,2,0,1:T(8,128)(2,1)}, u32[]{:S(2)}, u32[]{:S(2)}) %all-to-all-start.1) | async-done | bytes 5505056 | tf_op jit(solution)/shard_map/all_to_all | solution.py:77
  105.4 1.7 constant_dynamic-slice_fusion.1
  107.4 0.2 fusion.49
  107.5 4.5 select_reduce_fusion
  112.1 0.1 copy.79
  112.3 0.1 copy.80
  112.4 1.2 gather_fusion.2
  113.6 1.2 gather_fusion.1
  114.7 4.6 fusion.31
  119.3 0.1 broadcast_select_fusion.1
  119.4 0.1 broadcast_select_fusion.3
  119.6 0.1 pad_maximum_fusion.4
  119.7 24.5 %all_to_all.20 = bf16[16,16,896]{2,1,0:T(8,128)(2,1)S(1)} all-to-all(bf16[16,16,896]{2,1,0:T(8,128)(2,1)S(1)} %pad_maximum_fusion.4), channel_id=1, replica_groups=mesh['dp'=16,'expert'=16] {'dp'}, dimensions={0} | all-to-all | bytes 917504 | tf_op jit(solution)/shard_map/all_to_all | solution.py:88
  144.2 0.1 fusion.99
  144.4 0.1 maximum_bitcast_fusion
  144.5 1.0 pad_maximum_fusion.3
  145.5 0.2 reduce-scatter.2.cloned.1.call-start
  146.0 0.1 squeeze.52
  146.1 2.4 gather_fusion
  148.5 0.1 dynamic-slice_bitcast_fusion
  148.6 34.6 %all-gather.10.cloned.1.call-done = bf16[3,1,7168,128]{3,2,0,1:T(8,128)(2,1)} async-done(((bf16[3,1,448,128]{3,2,0,1:T(8,128)(2,1)}), bf16[3,1,7168,128]{3,2,0,1:T(8,128)(2,1)}) %all-gather.10.cloned.1.call-update) | async-done | bytes 5505040 | tf_op jit(solution)/shard_map/all_gather | solution.py:79
  183.1 5.2 fusion.98
  188.3 138.0 %all-gather.8.cloned.1.call-done = bf16[2,6144,448]{2,1,0:T(8,128)(2,1)} async-done(((bf16[2,384,448]{2,1,0:T(8,128)(2,1)}), bf16[2,6144,448]{2,1,0:T(8,128)(2,1)}) %all-gather.8.cloned.1.call-update) | async-done | bytes 11010064 | tf_op jit(solution)/shard_map/all_gather | solution.py:94
  326.3 5.4 fusion.96
  331.7 0.7 fusion.53
  332.4 2.2 copy-done.6
  334.6 0.7 fusion.56
  335.3 1.2 copy-done.7
  336.5 0.7 multiply_convert_fusion.5
  337.2 0.6 fusion.85
  337.8 1.2 fusion.40
  339.1 0.3 copy-done.5
  339.3 1.2 fusion.43
  340.6 0.3 copy-done.3
  340.8 1.2 multiply_convert_fusion.2
  342.1 1.1 fusion.73
  343.2 0.6 fusion.32
  343.8 1.2 fusion.5
  345.0 3.3 pad_maximum_fusion.2
  348.3 0.3 all-gather.6.cloned.1.call-start
  348.5 2.3 convert_bitcast_fusion.2
  350.9 2.3 convert_bitcast_fusion.1
  353.2 2.4 convert_bitcast_fusion
  355.6 0.9 pad_maximum_fusion.1
  356.5 0.4 copy.88
  356.9 121.3 %all_to_all.21 = bf16[3,16,448,128]{3,2,0,1:T(8,128)(2,1)} all-to-all(bf16[3,16,448,128]{3,2,0,1:T(8,128)(2,1)S(1)} %copy.88), channel_id=1, replica_groups=mesh['dp'=16,'expert'=16] {'dp'}, dimensions={1} | all-to-all | bytes 11010048 | tf_op jit(solution)/shard_map/all_to_all | solution.py:102
  478.2 4.3 reduce_sum.42
  482.5 0.1 and.35
  482.6 3.6 fusion.19
  486.2 4.9 fusion.22
  491.1 1.0 slice.123
  492.0 0.8 copy.92
  492.9 4.7 all-to-all-start.3
  497.6 4.8 fusion.16
  502.4 4.3 all-to-all-done.3
  506.7 1.8 fusion.39
  508.5 34.8 %all-gather.6.cloned.1.call-done = bf16[3,7168,128]{2,1,0:T(8,128)(2,1)} async-done(((bf16[3,448,128]{2,1,0:T(8,128)(2,1)}), bf16[3,7168,128]{2,1,0:T(8,128)(2,1)}) %all-gather.6.cloned.1.call-update) | async-done | bytes 5505040 | tf_op jit(solution)/shard_map/all_gather | solution.py:104
  543.3 5.1 fusion
  548.4 2.2 fusion.97
  550.5 2.9 copy.91
  (46 shorter events, 0.7 us)
Async XLA Ops:
  7.2 4.0 copy-start.2
  17.1 8.6 %copy-start.12 = (s32[16]{0:T(128)S(1)}, s32[16]{0:T(128)}, u32[]{:S(2)}) copy-start(s32[16]{0:T(128)} %param.17) | copy-start | bytes 196
  17.1 90.2 %copy-start.10 = (s32[2048,2]{0,1:T(2,128)S(1)}, s32[2048,2]{0,1:T(2,128)}, u32[]{:S(2)}) copy-start(s32[2048,2]{0,1:T(2,128)} %param.15) | copy-start | bytes 49156
  17.1 95.0 %copy-start.8 = (bf16[128,448]{0,1:T(8,128)(2,1)S(1)}, bf16[128,448]{0,1:T(8,128)(2,1)}, u32[]{:S(2)}) copy-start(bf16[128,448]{0,1:T(8,128)(2,1)} %param.11) | copy-start | bytes 344068
  17.1 95.1 %copy-start.9 = (bf16[128,448]{0,1:T(8,128)(2,1)S(1)}, bf16[128,448]{0,1:T(8,128)(2,1)}, u32[]{:S(2)}) copy-start(bf16[128,448]{0,1:T(8,128)(2,1)} %param.10) | copy-start | bytes 344068
  17.1 88.3 %all-to-all-start.1 = ((bf16[3,16,448,128]{3,2,0,1:T(8,128)(2,1)}), bf16[3,16,448,128]{3,2,0,1:T(8,128)(2,1)}, u32[]{:S(2)}, u32[]{:S(2)}) async-start(bf16[3,16,448,128]{3,2,0,1:T(8,128)(2,1)} %copy.87), calls=%async_computation.1 | async-start | bytes 11010048 | tf_op jit(solution)/shard_map/all_to_all | solution.py:77
  25.7 157.4 %all-gather.10.cloned.1.call-start = ((), (), s32[]{:S(2)}) async-start(), calls=%async_computation.8 | async-start | bytes 5849088 | tf_op jit(solution)/shard_map/all_gather | solution.py:79
  107.2 219.1 %all-gather.8.cloned.1.call-start = ((), (), s32[]{:S(2)}) async-start(), calls=%async_computation.7 | async-start | bytes 13369344 | tf_op jit(solution)/shard_map/all_gather | solution.py:94
  119.5 26.5 %copy-start.11 = (f32[2048,2]{0,1:T(2,128)S(1)}, f32[2048,2]{0,1:T(2,128)}, u32[]{:S(2)}) copy-start(f32[2048,2]{0,1:T(2,128)} %param.16) | copy-start | bytes 49156
  145.5 345.6 %reduce-scatter.2.cloned.1.call-start = ((), (), s32[]{:S(2)}) async-start(), calls=%async_computation.6 | async-start | bytes 5849088 | tf_op jit(solution)/shard_map/reduce_scatter | solution.py:115
  326.3 5.4 copy-start.4
  331.7 7.4 %copy-start = (bf16[1,6144,448]{2,1,0:T(8,128)(2,1)}, bf16[1,6144,448]{2,1,0:T(8,128)(2,1)S(1)}, u32[]{:S(2)}) copy-start(bf16[1,6144,448]{2,1,0:T(8,128)(2,1)S(1)} %get-tuple-element.5) | copy-start | bytes 16515076
  331.7 8.9 %copy-start.1 = (bf16[1,6144,448]{2,1,0:T(8,128)(2,1)}, bf16[1,6144,448]{2,1,0:T(8,128)(2,1)S(1)}, u32[]{:S(2)}) copy-start(bf16[1,6144,448]{2,1,0:T(8,128)(2,1)S(1)} %get-tuple-element.6) | copy-start | bytes 16515076
  331.7 2.9 copy-start.6
  331.7 4.8 copy-start.7
  337.8 1.5 copy-start.5
  339.3 1.5 copy-start.3
  348.3 195.0 %all-gather.6.cloned.1.call-start = ((), (), s32[]{:S(2)}) async-start(), calls=%async_computation.5 | async-start | bytes 5849088 | tf_op jit(solution)/shard_map/all_gather | solution.py:104
  492.9 13.8 %all-to-all-start.3 = ((bf16[16,16,448]{2,1,0:T(8,128)(2,1)}), bf16[16,16,448]{2,1,0:T(8,128)(2,1)S(1)}, u32[]{:S(2)}, u32[]{:S(2)}) async-start(bf16[16,16,448]{2,1,0:T(8,128)(2,1)} %bitcast.53), calls=%async_computation.4 | async-start | bytes 524288 | tf_op jit(solution)/shard_map/all_to_all | solution.py:120
Sparse Core Ops, SparseCore 0:
  107.3 75.7 all-gather.9
  184.9 141.3 all-gather.7
  348.4 114.3 reduce-scatter.1
  482.6 60.6 all-gather.5

commit v5 on v4

--- a/solution.py
+++ b/solution.py
@@ -71,12 +71,6 @@
     block_weight = lax.dynamic_slice_in_dim(route_weight, row_index * block_rows, block_rows, 0)
     hot_weight = block_weight[:, hot_expert]
 
-    share_count = lax.axis_size("expert")
-    own = jnp.stack([w_gate[0], w_up[0], w_down[0].T], 0)
-    own = own.reshape(3, share_count, width // share_count, own.shape[-1])
-    pieces = lax.all_to_all(own, "dp", split_axis=1, concat_axis=1, tiled=True)
-    hot_piece = lax.dynamic_index_in_dim(pieces, hot_expert, axis=1, keepdims=False)
-    hot_w = lax.all_gather(hot_piece, "dp", axis=1, tiled=True).reshape(own.shape)
 
     def pack(source):
         picked = jnp.take(source, send_token.reshape(-1), axis=0).reshape(
@@ -91,7 +85,15 @@
     local = jnp.stack(
         [jnp.concatenate([tokens, arrived_in], 0), jnp.concatenate([grad_out, arrived_back], 0)], 0
     )
+    share_count = lax.axis_size("expert")
+    own = jnp.stack([w_gate[0], w_up[0], w_down[0].T], 0)
+    own = own.reshape(3, share_count, width // share_count, own.shape[-1])
+    own, local = lax.optimization_barrier((own, local))
+    pieces = lax.all_to_all(own, "dp", split_axis=1, concat_axis=1, tiled=True)
+    hot_piece = lax.dynamic_index_in_dim(pieces, hot_expert, axis=1, keepdims=False)
     full = lax.all_gather(local, "expert", axis=1)
+    hot_piece, full = lax.optimization_barrier((hot_piece, full))
+    hot_w = lax.all_gather(hot_piece, "dp", axis=1, tiled=True).reshape(own.shape)
     full_in, full_back = full[0], full[1]
     hot_rows, cold_rows = (full_in[:, :block_rows], full_in[:, block_rows:])
     hot_cotan, cold_cotan = (full_back[:, :block_rows], full_back[:, block_rows:])

time: 561 us -> 555 us (0.989)
  waiting for transfers between devices: 291 us -> 256 us
  local copies, waits for them, and re-layouts: 35.8 us -> 67.2 us
  blocking collectives: 146 us -> 122 us
  matrix products: 31.6 us -> 42.6 us
    all_gather x1, waiting for transfers between devices: 138 us -> 0.01 us  [on_device(): full = lax.all_gather(local, 'expert', axis=1)]
    all_to_all x1, waiting for transfers between devices: 79.6 us -> 189 us  [on_device(): pieces = lax.all_to_all(own, 'dp', split_axis=1, concat_axis=1, tiled=True)]
    all_to_all x1 -> x0, blocking collectives: 24.5 us -> none  [on_device(): lax.all_to_all(packed, 'dp', split_axis=0, concat_axis=0, tiled=True)]
    optimization_barrier x0 -> x2, local copies, waits for them, and re-layouts: none -> 17 us  [the longest x1 11.7 us: on_device(): hot_piece, full = lax.optimization_barrier((hot_piece, full))]
    all_gather x0 -> x1, local copies, waits for them, and re-layouts: none -> 16.5 us  [on_device(): full = lax.all_gather(local, 'expert', axis=1)]
    squeeze x0 -> x2, local copies, waits for them, and re-layouts: none -> 11.2 us  [the longest x1 9.46 us: on_device(): full_in, full_back = (full[0], full[1])]
    all_gather x1, waiting for transfers between devices: 34.6 us -> 24.5 us  [on_device(): lax.all_gather(hot_piece, 'dp', axis=1, tiled=True).reshape(own.shape)]
    all_to_all x0 -> x1, starting transfers between devices: none -> 8.43 us  [on_device(): lax.all_to_all(packed, 'dp', split_axis=0, concat_axis=0, tiled=True)]
  transfers between devices with their start and end apart: 6 -> 7, of which waited for: 5 -> 5; matrix products, arithmetic and copies ran while one was open for 9% -> 15% of each run, Pallas kernels for 0% -> 0%
where the time goes in v5:
time: 555 us; the launch traced here: 553 us
  waiting for transfers between devices  256 us (46%)
  blocking collectives  122 us (22%)
  local copies, waits for them, and re-layouts  67.2 us (12%)
  matrix products  42.6 us (8%)
  other arithmetic  31.4 us (6%)
  starting transfers between devices  19.2 us (3%)
  between operations  14.2 us (3%)
    all_to_all x1, waiting for transfers between devices, on_device(): pieces = lax.all_to_all(own, 'dp', split_axis=1, concat_axis=1, tiled=True)  189 us
    all_to_all x1, blocking collectives, on_device(): lax.all_to_all(block_sums, 'dp', split_axis=1, concat_axis=1, tiled=True)  122 us
    all_gather x1, waiting for transfers between devices, on_device(): lax.all_gather(chunk_sum, 'dp', axis=1, tiled=True)  35.2 us
    all_gather x1, waiting for transfers between devices, on_device(): lax.all_gather(hot_piece, 'dp', axis=1, tiled=True).reshape(own.shape)  24.5 us
    all_gather x1, local copies, waits for them, and re-layouts, on_device(): full = lax.all_gather(local, 'expert', axis=1)  16.5 us
    optimization_barrier x1, local copies, waits for them, and re-layouts, on_device(): hot_piece, full = lax.optimization_barrier((hot_piece, full))  11.7 us
  transfers between devices with their start and end apart: 7, of which 5 were waited for; matrix products, arithmetic and copies ran while one was open for 15% of the time, Pallas kernels for 0%

profile of v5, /device:TPU:1, one launch (start us, length us, event | category | flops | bytes accessed | tf_op | source)
XLA Modules:
  0.0 553.0 jit_solution(15930618665952894577)
XLA Ops:
  7.2 0.8 convert_reduce_fusion
  8.0 0.2 fusion.63
  8.1 0.7 iota_compare_fusion.4
  8.8 4.6 fusion.32
  13.4 4.5 select_reduce_fusion
  18.0 1.0 copy.72
  19.0 1.0 copy.71
  20.0 1.2 gather_fusion.2
  21.2 1.2 gather_fusion.1
  22.3 0.1 broadcast_select_fusion.1
  22.5 0.1 broadcast_select_fusion.3
  22.6 0.9 pad_maximum_fusion.4
  23.5 8.4 %all-to-all-start = ((bf16[16,16,896]{2,1,0:T(8,128)(2,1)}), bf16[16,16,896]{2,1,0:T(8,128)(2,1)S(1)}, u32[]{:S(2)}, u32[]{:S(2)}) async-start(bf16[16,16,896]{2,1,0:T(8,128)(2,1)} %pad_maximum_fusion.4), calls=%async_computation | async-start | bytes 917504 | tf_op jit(solution)/shard_map/all_to_all | solution.py:82
  32.0 3.3 copy.67
  35.3 5.1 pad_maximum_fusion
  40.4 2.2 all-to-all-done
  42.6 0.1 fusion.113
  42.7 0.1 maximum_bitcast_fusion
  42.8 1.0 pad_maximum_fusion.3
  43.8 5.4 copy.74
  49.2 5.5 all-to-all-start.1
  54.9 189.4 %all-to-all-done.1 = bf16[3,16,448,128]{3,2,0,1:T(8,128)(2,1)} async-done(((bf16[3,16,448,128]{3,2,0,1:T(8,128)(2,1)}), bf16[3,16,448,128]{3,2,0,1:T(8,128)(2,1)}, u32[]{:S(2)}, u32[]{:S(2)}) %all-to-all-start.1) | async-done | bytes 5505056 | tf_op jit(solution)/shard_map/all_to_all | solution.py:92
  244.2 1.7 dynamic-slice_bitcast_fusion
  246.0 16.5 %copy.81 = bf16[2,16,384,448]{2,1,3,0:T(8,128)(2,1)} copy(bf16[2,16,384,448]{3,2,1,0:T(8,128)(2,1)} %bitcast.156) | data formatting | bytes 22020096 | tf_op jit(solution)/shard_map/all_gather | solution.py:94
  262.6 0.1 squeeze.52
  262.9 2.4 gather_fusion
  265.4 11.7 %copy.76 = bf16[2,16,384,448]{2,3,1,0:T(8,128)(2,1)} copy(bf16[2,16,384,448]{2,1,3,0:T(8,128)(2,1)} %copy.81) | data formatting | bytes 22020096 | tf_op jit(solution)/shard_map/optimization_barrier | solution.py:95
  277.1 9.5 %slice_bitcast_fusion.1 = (bf16[16,384,448]{1,2,0:T(8,128)(2,1)}, bf16[16,384,448]{1,2,0:T(8,128)(2,1)}) fusion(bf16[2,16,384,448]{2,3,1,0:T(8,128)(2,1)} %copy.76), kind=kLoop, calls=%fused_computation.7 | loop fusion | bytes 22020096 | tf_op jit(solution)/shard_map/squeeze | solution.py:97
  286.5 3.9 fusion.53
  290.5 0.3 copy-done
  290.7 2.9 fusion.48
  293.7 3.2 multiply_convert_fusion.2
  296.9 1.1 fusion.25
  298.0 3.0 fusion.1
  301.0 24.5 %all-gather.5.cloned.1.call-done = bf16[3,7168,128]{2,1,0:T(8,128)(2,1)} async-done(((bf16[3,448,128]{2,1,0:T(8,128)(2,1)}), bf16[3,7168,128]{2,1,0:T(8,128)(2,1)}) %all-gather.5.cloned.1.call-update) | async-done | bytes 5505040 | tf_op jit(solution)/shard_map/all_gather | solution.py:96
  325.6 3.0 fusion.112
  328.5 2.2 fusion.72
  330.8 2.2 fusion.69
  333.0 2.2 multiply_convert_fusion.5
  335.2 0.6 fusion.100
  335.9 0.6 fusion.40
  336.5 1.4 copy-done.1
  337.9 3.3 pad_maximum_fusion.2
  341.2 0.3 all-gather.7.cloned.1.call-start
  341.5 2.1 convert_bitcast_fusion.1
  343.6 2.1 convert_bitcast_fusion.2
  345.7 2.2 convert_bitcast_fusion
  347.9 0.9 pad_maximum_fusion.1
  348.8 0.4 copy.78
  349.2 122.2 %all_to_all.20 = bf16[3,16,448,128]{3,2,0,1:T(8,128)(2,1)} all-to-all(bf16[3,16,448,128]{3,2,0,1:T(8,128)(2,1)S(1)} %copy.78), channel_id=1, replica_groups=mesh['dp'=16,'expert'=16] {'dp'}, dimensions={1} | all-to-all | bytes 11010048 | tf_op jit(solution)/shard_map/all_to_all | solution.py:104
  471.4 4.3 reduce_sum.42
  475.8 0.1 and.35
  475.8 3.1 fusion.16
  479.0 4.5 fusion.22
  483.5 1.0 slice.124
  484.4 0.8 copy.80
  485.3 4.8 all-to-all-start.3
  490.1 4.4 fusion.19
  494.5 4.9 all-to-all-done.3
  499.4 1.8 fusion.47
  501.2 35.2 %all-gather.7.cloned.1.call-done = bf16[3,7168,128]{2,1,0:T(8,128)(2,1)} async-done(((bf16[3,448,128]{2,1,0:T(8,128)(2,1)}), bf16[3,7168,128]{2,1,0:T(8,128)(2,1)}) %all-gather.7.cloned.1.call-update) | async-done | bytes 5505040 | tf_op jit(solution)/shard_map/all_gather | solution.py:106
  536.4 5.1 fusion
  541.4 2.2 fusion.111
  543.6 2.9 copy.79
  (38 shorter events, 0.7 us)
Async XLA Ops:
  23.5 19.1 %all-to-all-start = ((bf16[16,16,896]{2,1,0:T(8,128)(2,1)}), bf16[16,16,896]{2,1,0:T(8,128)(2,1)S(1)}, u32[]{:S(2)}, u32[]{:S(2)}) async-start(bf16[16,16,896]{2,1,0:T(8,128)(2,1)} %pad_maximum_fusion.4), calls=%async_computation | async-start | bytes 917504 | tf_op jit(solution)/shard_map/all_to_all | solution.py:82
  31.9 214.1 %all-gather.9.cloned.1.call-start = ((), (), s32[]{:S(2)}) async-start(), calls=%async_computation.8 | async-start | bytes 13369344 | tf_op jit(solution)/shard_map/all_gather | solution.py:94
  49.2 5.6 %copy-start.4 = (s32[16]{0:T(128)S(1)}, s32[16]{0:T(128)}, u32[]{:S(2)}) copy-start(s32[16]{0:T(128)} %param.17) | copy-start | bytes 196
  49.2 195.0 %all-to-all-start.1 = ((bf16[3,16,448,128]{3,2,0,1:T(8,128)(2,1)}), bf16[3,16,448,128]{3,2,0,1:T(8,128)(2,1)}, u32[]{:S(2)}, u32[]{:S(2)}) async-start(bf16[3,16,448,128]{3,2,0,1:T(8,128)(2,1)} %copy.74), calls=%async_computation.1 | async-start | bytes 11010048 | tf_op jit(solution)/shard_map/all_to_all | solution.py:92
  54.7 270.9 %all-gather.5.cloned.1.call-start = ((), (), s32[]{:S(2)}) async-start(), calls=%async_computation.5 | async-start | bytes 5849088 | tf_op jit(solution)/shard_map/all_gather | solution.py:96
  246.0 16.9 %copy-start.2 = (s32[2048,2]{0,1:T(2,128)S(1)}, s32[2048,2]{0,1:T(2,128)}, u32[]{:S(2)}) copy-start(s32[2048,2]{0,1:T(2,128)} %param.15) | copy-start | bytes 49156
  246.0 16.9 %copy-start.3 = (f32[2048,2]{0,1:T(2,128)S(1)}, f32[2048,2]{0,1:T(2,128)}, u32[]{:S(2)}) copy-start(f32[2048,2]{0,1:T(2,128)} %param.16) | copy-start | bytes 49156
  262.5 220.9 %reduce-scatter.2.cloned.1.call-start = ((), (), s32[]{:S(2)}) async-start(), calls=%async_computation.7 | async-start | bytes 5849088 | tf_op jit(solution)/shard_map/reduce_scatter | solution.py:117
  286.5 4.2 copy-start
  286.5 7.1 %slice-start = ((s8[5505024]{0:T(1024)(128)(4,1)}), s8[4194304]{0:T(1024)(128)(4,1)S(1)}, s32[]{:S(2)}) async-start(s8[5505024]{0:T(1024)(128)(4,1)} %bitcast.154), calls=%async_computation.9 | async-start | bytes 8388608
  290.7 2.9 slice-start.1
  335.9 2.0 copy-start.1
  341.2 195.2 %all-gather.7.cloned.1.call-start = ((), (), s32[]{:S(2)}) async-start(), calls=%async_computation.6 | async-start | bytes 5849088 | tf_op jit(solution)/shard_map/all_gather | solution.py:106
  485.3 14.1 %all-to-all-start.3 = ((bf16[16,16,448]{2,1,0:T(8,128)(2,1)}), bf16[16,16,448]{2,1,0:T(8,128)(2,1)S(1)}, u32[]{:S(2)}, u32[]{:S(2)}) async-start(bf16[16,16,448]{2,1,0:T(8,128)(2,1)} %bitcast.54), calls=%async_computation.4 | async-start | bytes 524288 | tf_op jit(solution)/shard_map/all_to_all | solution.py:122
Sparse Core Ops, SparseCore 0:
  44.0 187.5 all-gather.8
  262.6 62.9 all-gather.4
  341.3 114.5 reduce-scatter.1
  475.8 60.5 all-gather.6

commit v6 on v3

--- a/solution.py
+++ b/solution.py
@@ -76,7 +76,8 @@
     own = own.reshape(3, share_count, width // share_count, own.shape[-1])
     pieces = lax.all_to_all(own, "dp", split_axis=1, concat_axis=1, tiled=True)
     hot_piece = lax.dynamic_index_in_dim(pieces, hot_expert, axis=1, keepdims=False)
-    hot_w = lax.all_gather(hot_piece, "dp", axis=1, tiled=True).reshape(own.shape)
+    copies = jnp.broadcast_to(hot_piece[:, None], own.shape)
+    hot_w = lax.all_to_all(copies, "dp", split_axis=1, concat_axis=1, tiled=True)
 
     def pack(source):
         picked = jnp.take(source, send_token.reshape(-1), axis=0).reshape(

time: 544 us -> 534 us (0.982)
  waiting for transfers between devices: 275 us -> 260 us
    all_gather x1 -> x0, waiting for transfers between devices: 62 us -> none  [on_device(): lax.all_gather(hot_piece, 'dp', axis=1, tiled=True).reshape(own.shape)]
    all_to_all x0 -> x1, waiting for transfers between devices: none -> 24.4 us  [on_device(): lax.all_to_all(copies, 'dp', split_axis=1, concat_axis=1, tiled=True)]
    all_gather x1, waiting for transfers between devices: 51.5 us -> 72.7 us  [on_device(): lax.all_gather(jnp.concatenate([grad_out, arrived_back], 0), 'expert', ax...]
  transfers between devices with their start and end apart: 7 -> 7, of which waited for: 5 -> 5; matrix products, arithmetic and copies ran while one was open for 11% -> 12% of each run, Pallas kernels for 0% -> 0%
where the time goes in v6:
time: 534 us; the launch traced here: 533 us
  waiting for transfers between devices  260 us (49%)
  blocking collectives  138 us (26%)
  matrix products  49.7 us (9%)
  other arithmetic  29.1 us (5%)
  local copies, waits for them, and re-layouts  26.8 us (5%)
  starting transfers between devices  15.6 us (3%)
  between operations  14.2 us (3%)
    all_to_all x1, waiting for transfers between devices, on_device(): pieces = lax.all_to_all(own, 'dp', split_axis=1, concat_axis=1, tiled=True)  122 us
    all_to_all x1, blocking collectives, on_device(): lax.all_to_all(block_sums, 'dp', split_axis=1, concat_axis=1, tiled=True)  119 us
    all_gather x1, waiting for transfers between devices, on_device(): lax.all_gather(jnp.concatenate([grad_out, arrived_back], 0), 'expert', ax...  72.7 us
    all_gather x1, waiting for transfers between devices, on_device(): lax.all_gather(chunk_sum, 'dp', axis=1, tiled=True)  35.6 us
    all_to_all x1, waiting for transfers between devices, on_device(): lax.all_to_all(copies, 'dp', split_axis=1, concat_axis=1, tiled=True)  24.4 us
    all_to_all x1, blocking collectives, on_device(): lax.all_to_all(packed, 'dp', split_axis=0, concat_axis=0, tiled=True)  19 us
  transfers between devices with their start and end apart: 7, of which 5 were waited for; matrix products, arithmetic and copies ran while one was open for 12% of the time, Pallas kernels for 0%

profile of v6, /device:TPU:1, one launch (start us, length us, event | category | flops | bytes accessed | tf_op | source)
XLA Modules:
  0.0 533.1 jit_solution(14729485854908545992)
XLA Ops:
  7.2 0.8 convert_reduce_fusion
  8.0 0.2 fusion.50
  8.2 0.7 iota_compare_fusion.4
  8.8 4.5 select_reduce_fusion
  13.5 4.6 fusion.31
  18.0 1.0 copy.84
  19.0 1.0 copy.85
  20.0 1.2 gather_fusion.2
  21.2 1.2 gather_fusion.1
  22.4 0.1 broadcast_select_fusion.1
  22.5 0.1 broadcast_select_fusion.3
  22.6 0.1 pad_maximum_fusion.3
  22.8 19.0 %all_to_all.25 = bf16[16,16,896]{2,1,0:T(8,128)(2,1)S(1)} all-to-all(bf16[16,16,896]{2,1,0:T(8,128)(2,1)S(1)} %pad_maximum_fusion.3), channel_id=1, replica_groups=mesh['dp'=16,'expert'=16] {'dp'}, dimensions={0} | all-to-all | bytes 917504 | tf_op jit(solution)/shard_map/all_to_all | solution.py:89
  41.8 0.1 fusion.97
  41.9 0.8 pad_maximum_fusion.4
  42.8 0.8 pad_maximum_fusion.5
  43.6 3.9 copy.91
  47.5 3.1 pad_maximum_fusion
  50.6 2.8 copy.92
  53.4 5.5 %all-to-all-start.1 = ((bf16[3,16,448,128]{3,2,0,1:T(8,128)(2,1)}), bf16[3,16,448,128]{3,2,0,1:T(8,128)(2,1)}, u32[]{:S(2)}, u32[]{:S(2)}) async-start(bf16[3,16,448,128]{3,2,0,1:T(8,128)(2,1)} %copy.92), calls=%async_computation.1 | async-start | bytes 11010048 | tf_op jit(solution)/shard_map/all_to_all | solution.py:77
  59.0 122.5 %all-to-all-done.1 = bf16[3,16,448,128]{3,2,0,1:T(8,128)(2,1)} async-done(((bf16[3,16,448,128]{3,2,0,1:T(8,128)(2,1)}), bf16[3,16,448,128]{3,2,0,1:T(8,128)(2,1)}, u32[]{:S(2)}, u32[]{:S(2)}) %all-to-all-start.1) | async-done | bytes 5505056 | tf_op jit(solution)/shard_map/all_to_all | solution.py:77
  181.5 1.0 dynamic-slice_bitcast_fusion
  182.5 3.7 broadcast_in_dim.81
  186.2 4.9 all-to-all-start.2
  191.1 0.2 reduce-scatter.2.cloned.1.call-start
  191.6 0.1 squeeze.41
  191.7 2.4 gather_fusion
  194.1 0.1 dynamic-slice_bitcast_fusion.1
  194.2 3.6 fusion.41
  197.8 0.6 copy-done
  198.4 2.7 fusion.44
  201.1 72.7 %all-gather.10.cloned.1.call-done = bf16[6144,448]{1,0:T(8,128)(2,1)} async-done(((bf16[384,448]{1,0:T(8,128)(2,1)}), bf16[6144,448]{1,0:T(8,128)(2,1)}) %all-gather.10.cloned.1.call-update) | async-done | bytes 5505040 | tf_op jit(solution)/shard_map/all_gather | solution.py:93
  273.8 4.0 multiply_convert_fusion.2
  277.8 1.1 fusion.74
  279.0 3.0 fusion.5
  282.0 24.4 %all-to-all-done.2 = bf16[3,16,448,128]{3,2,0,1:T(8,128)(2,1)} async-done(((bf16[3,16,448,128]{3,2,0,1:T(8,128)(2,1)}), bf16[3,16,448,128]{3,2,0,1:T(8,128)(2,1)}, u32[]{:S(2)}, u32[]{:S(2)}) %all-to-all-start.2) | async-done | bytes 5505056 | tf_op jit(solution)/shard_map/all_to_all | solution.py:80
  306.4 2.8 fusion.54
  309.2 2.8 fusion.57
  312.0 2.8 multiply_convert_fusion.5
  314.9 2.1 fusion.33
  317.0 2.3 fusion.35
  319.3 0.3 copy-done.1
  319.6 3.2 pad_maximum_fusion.2
  322.9 0.3 all-gather.6.cloned.1.call-start
  323.2 2.3 convert_bitcast_fusion.2
  325.5 2.3 convert_bitcast_fusion.1
  327.8 2.4 convert_bitcast_fusion
  330.2 0.9 pad_maximum_fusion.1
  331.1 0.4 copy.96
  331.5 118.7 %all_to_all.26 = bf16[3,16,448,128]{3,2,0,1:T(8,128)(2,1)} all-to-all(bf16[3,16,448,128]{3,2,0,1:T(8,128)(2,1)S(1)} %copy.96), channel_id=1, replica_groups=mesh['dp'=16,'expert'=16] {'dp'}, dimensions={1} | all-to-all | bytes 11010048 | tf_op jit(solution)/shard_map/all_to_all | solution.py:100
  450.2 4.3 reduce_sum.42
  454.5 0.1 and.35
  454.6 3.6 fusion.19
  458.2 4.9 fusion.22
  463.1 1.0 slice.105
  464.0 0.9 copy.100
  464.9 4.7 all-to-all-start.4
  469.6 4.8 fusion.16
  474.4 4.7 all-to-all-done.4
  479.1 1.8 fusion.40
  480.9 35.6 %all-gather.6.cloned.1.call-done = bf16[3,7168,128]{2,1,0:T(8,128)(2,1)} async-done(((bf16[3,448,128]{2,1,0:T(8,128)(2,1)}), bf16[3,7168,128]{2,1,0:T(8,128)(2,1)}) %all-gather.6.cloned.1.call-update) | async-done | bytes 5505040 | tf_op jit(solution)/shard_map/all_gather | solution.py:102
  516.5 5.1 fusion
  521.6 2.2 fusion.96
  523.7 2.9 copy.99
  (35 shorter events, 0.6 us)
Async XLA Ops:
  7.2 187.0 %all-gather.8.cloned.1.call-start = ((), (), s32[]{:S(2)}) async-start(), calls=%async_computation.8 | async-start | bytes 6684672 | tf_op jit(solution)/shard_map/all_gather | solution.py:92
  22.7 24.8 %copy-start.2 = (bf16[1,7168,128]{2,1,0:T(8,128)(2,1)S(1)}, bf16[1,7168,128]{2,1,0:T(8,128)(2,1)}, u32[]{:S(2)}) copy-start(bf16[1,7168,128]{2,1,0:T(8,128)(2,1)} %param.13) | copy-start | bytes 5505028
  42.8 231.0 %all-gather.10.cloned.1.call-start = ((), (), s32[]{:S(2)}) async-start(), calls=%async_computation.9 | async-start | bytes 6684672 | tf_op jit(solution)/shard_map/all_gather | solution.py:93
  53.4 5.5 %copy-start.6 = (s32[16]{0:T(128)S(1)}, s32[16]{0:T(128)}, u32[]{:S(2)}) copy-start(s32[16]{0:T(128)} %param.17) | copy-start | bytes 196
  53.4 128.1 %all-to-all-start.1 = ((bf16[3,16,448,128]{3,2,0,1:T(8,128)(2,1)}), bf16[3,16,448,128]{3,2,0,1:T(8,128)(2,1)}, u32[]{:S(2)}, u32[]{:S(2)}) async-start(bf16[3,16,448,128]{3,2,0,1:T(8,128)(2,1)} %copy.92), calls=%async_computation.1 | async-start | bytes 11010048 | tf_op jit(solution)/shard_map/all_to_all | solution.py:77
  186.2 5.5 %copy-start.4 = (s32[2048,2]{0,1:T(2,128)S(1)}, s32[2048,2]{0,1:T(2,128)}, u32[]{:S(2)}) copy-start(s32[2048,2]{0,1:T(2,128)} %param.15) | copy-start | bytes 49156
  186.2 5.5 %copy-start.5 = (f32[2048,2]{0,1:T(2,128)S(1)}, f32[2048,2]{0,1:T(2,128)}, u32[]{:S(2)}) copy-start(f32[2048,2]{0,1:T(2,128)} %param.16) | copy-start | bytes 49156
  186.2 120.1 %all-to-all-start.2 = ((bf16[3,16,448,128]{3,2,0,1:T(8,128)(2,1)}), bf16[3,16,448,128]{3,2,0,1:T(8,128)(2,1)}, u32[]{:S(2)}, u32[]{:S(2)}) async-start(bf16[3,16,448,128]{3,2,0,1:T(8,128)(2,1)} %broadcast_in_dim.81), calls=%async_computation.2 | async-start | bytes 11010048 | tf_op jit(solution)/shard_map/all_to_all | solution.py:80
  191.1 271.9 %reduce-scatter.2.cloned.1.call-start = ((), (), s32[]{:S(2)}) async-start(), calls=%async_computation.7 | async-start | bytes 5849088 | tf_op jit(solution)/shard_map/reduce_scatter | solution.py:113
  194.2 4.2 copy-start
  273.8 4.1 copy-start.3
  317.0 2.6 copy-start.1
  322.9 193.6 %all-gather.6.cloned.1.call-start = ((), (), s32[]{:S(2)}) async-start(), calls=%async_computation.6 | async-start | bytes 5849088 | tf_op jit(solution)/shard_map/all_gather | solution.py:102
  464.9 14.2 %all-to-all-start.4 = ((bf16[16,16,448]{2,1,0:T(8,128)(2,1)}), bf16[16,16,448]{2,1,0:T(8,128)(2,1)S(1)}, u32[]{:S(2)}, u32[]{:S(2)}) async-start(bf16[16,16,448]{2,1,0:T(8,128)(2,1)} %bitcast.52), calls=%async_computation.5 | async-start | bytes 524288 | tf_op jit(solution)/shard_map/all_to_all | solution.py:118
Sparse Core Ops, SparseCore 0:
  42.9 111.2 all-gather.7
  156.5 117.2 all-gather.9
  323.0 111.4 reduce-scatter.1
  454.6 61.8 all-gather.5

commit v7 on v4

--- a/solution.py
+++ b/solution.py
@@ -76,7 +76,8 @@
     own = own.reshape(3, share_count, width // share_count, own.shape[-1])
     pieces = lax.all_to_all(own, "dp", split_axis=1, concat_axis=1, tiled=True)
     hot_piece = lax.dynamic_index_in_dim(pieces, hot_expert, axis=1, keepdims=False)
-    hot_w = lax.all_gather(hot_piece, "dp", axis=1, tiled=True).reshape(own.shape)
+    copies = jnp.broadcast_to(hot_piece[:, None], own.shape)
+    hot_w = lax.all_to_all(copies, "dp", split_axis=1, concat_axis=1, tiled=True)
 
     def pack(source):
         picked = jnp.take(source, send_token.reshape(-1), axis=0).reshape(

time: 561 us -> 568 us (1.012)
  matrix products: 31.6 us -> 43.1 us
  waiting for transfers between devices: 291 us -> 283 us
    all_gather x1, waiting for transfers between devices: 138 us -> 0.01 us  [on_device(): full = lax.all_gather(local, 'expert', axis=1)]
    all_to_all x1, waiting for transfers between devices: 79.6 us -> 187 us  [on_device(): pieces = lax.all_to_all(own, 'dp', split_axis=1, concat_axis=1, tiled=True)]
    all_to_all x0 -> x1, waiting for transfers between devices: none -> 56.8 us  [on_device(): lax.all_to_all(copies, 'dp', split_axis=1, concat_axis=1, tiled=True)]
    all_gather x1 -> x0, waiting for transfers between devices: 34.6 us -> none  [on_device(): lax.all_gather(hot_piece, 'dp', axis=1, tiled=True).reshape(own.shape)]
    all_to_all x1, blocking collectives: 121 us -> 129 us  [on_device(): lax.all_to_all(block_sums, 'dp', split_axis=1, concat_axis=1, tiled=True)]
  transfers between devices with their start and end apart: 6 -> 6, of which waited for: 5 -> 4; matrix products, arithmetic and copies ran while one was open for 9% -> 11% of each run, Pallas kernels for 0% -> 0%
where the time goes in v7:
time: 568 us; the launch traced here: 567 us
  waiting for transfers between devices  283 us (50%)
  blocking collectives  148 us (26%)
  matrix products  43.1 us (8%)
  local copies, waits for them, and re-layouts  34.2 us (6%)
  other arithmetic  28.6 us (5%)
  starting transfers between devices  15.6 us (3%)
  between operations  14.3 us (3%)
    all_to_all x1, waiting for transfers between devices, on_device(): pieces = lax.all_to_all(own, 'dp', split_axis=1, concat_axis=1, tiled=True)  187 us
    all_to_all x1, blocking collectives, on_device(): lax.all_to_all(block_sums, 'dp', split_axis=1, concat_axis=1, tiled=True)  129 us
    all_to_all x1, waiting for transfers between devices, on_device(): lax.all_to_all(copies, 'dp', split_axis=1, concat_axis=1, tiled=True)  56.8 us
    all_gather x1, waiting for transfers between devices, on_device(): lax.all_gather(chunk_sum, 'dp', axis=1, tiled=True)  35.2 us
    all_to_all x1, blocking collectives, on_device(): lax.all_to_all(packed, 'dp', split_axis=0, concat_axis=0, tiled=True)  18.9 us
  transfers between devices with their start and end apart: 6, of which 4 were waited for; matrix products, arithmetic and copies ran while one was open for 11% of the time, Pallas kernels for 0%

profile of v7, /device:TPU:1, one launch (start us, length us, event | category | flops | bytes accessed | tf_op | source)
XLA Modules:
  0.0 566.5 jit_solution(7746942986209930433)
XLA Ops:
  7.2 0.8 convert_reduce_fusion
  8.0 0.2 fusion.50
  8.2 0.7 iota_compare_fusion.4
  8.8 4.5 select_reduce_fusion
  13.5 4.6 fusion.31
  18.0 1.0 copy.84
  19.0 1.0 copy.85
  20.0 1.2 gather_fusion.2
  21.2 1.2 gather_fusion.1
  22.4 0.1 broadcast_select_fusion.1
  22.5 0.1 broadcast_select_fusion.3
  22.6 0.1 pad_maximum_fusion.4
  22.7 18.9 %all_to_all.25 = bf16[16,16,896]{2,1,0:T(8,128)(2,1)S(1)} all-to-all(bf16[16,16,896]{2,1,0:T(8,128)(2,1)S(1)} %pad_maximum_fusion.4), channel_id=1, replica_groups=mesh['dp'=16,'expert'=16] {'dp'}, dimensions={0} | all-to-all | bytes 917504 | tf_op jit(solution)/shard_map/all_to_all | solution.py:89
  41.7 0.1 fusion.98
  41.8 0.1 maximum_bitcast_fusion
  41.9 1.0 pad_maximum_fusion.3
  42.9 3.9 copy.91
  46.8 3.1 pad_maximum_fusion
  49.9 2.8 copy.92
  52.7 5.5 all-to-all-start.1
  58.3 186.5 %all-to-all-done.1 = bf16[3,16,448,128]{3,2,0,1:T(8,128)(2,1)} async-done(((bf16[3,16,448,128]{3,2,0,1:T(8,128)(2,1)}), bf16[3,16,448,128]{3,2,0,1:T(8,128)(2,1)}, u32[]{:S(2)}, u32[]{:S(2)}) %all-to-all-start.1) | async-done | bytes 5505056 | tf_op jit(solution)/shard_map/all_to_all | solution.py:77
  244.9 1.0 dynamic-slice_bitcast_fusion
  245.9 3.7 broadcast_in_dim.81
  249.6 4.9 all-to-all-start.2
  254.5 0.2 reduce-scatter.2.cloned.1.call-start
  255.0 0.1 squeeze.49
  255.1 2.4 gather_fusion
  257.6 5.2 fusion.96
  262.9 1.3 fusion.41
  264.1 1.6 copy-done.5
  265.7 1.2 fusion.44
  267.0 1.2 copy-done.2
  268.2 1.2 multiply_convert_fusion.2
  269.4 1.1 fusion.74
  270.5 3.0 fusion.5
  273.5 56.8 %all-to-all-done.2 = bf16[3,16,448,128]{3,2,0,1:T(8,128)(2,1)} async-done(((bf16[3,16,448,128]{3,2,0,1:T(8,128)(2,1)}), bf16[3,16,448,128]{3,2,0,1:T(8,128)(2,1)}, u32[]{:S(2)}, u32[]{:S(2)}) %all-to-all-start.2) | async-done | bytes 5505056 | tf_op jit(solution)/shard_map/all_to_all | solution.py:80
  330.4 2.8 fusion.54
  333.2 2.8 fusion.57
  336.0 2.8 multiply_convert_fusion.5
  338.9 2.1 fusion.33
  341.0 2.3 fusion.35
  343.3 0.3 copy-done.1
  343.6 3.2 pad_maximum_fusion.2
  346.9 0.3 all-gather.4.cloned.1.call-start
  347.1 2.3 convert_bitcast_fusion.2
  349.5 2.3 convert_bitcast_fusion.1
  351.8 2.4 convert_bitcast_fusion
  354.2 0.9 pad_maximum_fusion.1
  355.1 0.4 copy.96
  355.5 128.7 %all_to_all.26 = bf16[3,16,448,128]{3,2,0,1:T(8,128)(2,1)} all-to-all(bf16[3,16,448,128]{3,2,0,1:T(8,128)(2,1)S(1)} %copy.96), channel_id=1, replica_groups=mesh['dp'=16,'expert'=16] {'dp'}, dimensions={1} | all-to-all | bytes 11010048 | tf_op jit(solution)/shard_map/all_to_all | solution.py:103
  484.1 4.3 reduce_sum.42
  488.5 0.1 and.35
  488.5 3.6 fusion.19
  492.1 4.9 fusion.22
  497.0 1.0 slice.117
  498.0 0.8 copy.100
  498.8 4.7 all-to-all-start.4
  503.5 4.8 fusion.16
  508.3 4.5 all-to-all-done.4
  512.8 1.8 fusion.40
  514.6 35.2 %all-gather.4.cloned.1.call-done = bf16[3,7168,128]{2,1,0:T(8,128)(2,1)} async-done(((bf16[3,448,128]{2,1,0:T(8,128)(2,1)}), bf16[3,7168,128]{2,1,0:T(8,128)(2,1)}) %all-gather.4.cloned.1.call-update) | async-done | bytes 5505040 | tf_op jit(solution)/shard_map/all_gather | solution.py:105
  549.9 5.1 fusion
  554.9 2.2 fusion.97
  557.1 2.9 copy.99
  (37 shorter events, 0.6 us)
Async XLA Ops:
  7.2 250.4 %all-gather.6.cloned.1.call-start = ((), (), s32[]{:S(2)}) async-start(), calls=%async_computation.8 | async-start | bytes 13369344 | tf_op jit(solution)/shard_map/all_gather | solution.py:95
  41.7 5.1 copy-start.3
  52.7 5.5 copy-start.8
  52.7 192.2 %all-to-all-start.1 = ((bf16[3,16,448,128]{3,2,0,1:T(8,128)(2,1)}), bf16[3,16,448,128]{3,2,0,1:T(8,128)(2,1)}, u32[]{:S(2)}, u32[]{:S(2)}) async-start(bf16[3,16,448,128]{3,2,0,1:T(8,128)(2,1)} %copy.92), calls=%async_computation.1 | async-start | bytes 11010048 | tf_op jit(solution)/shard_map/all_to_all | solution.py:77
  249.6 5.5 copy-start.6
  249.6 5.5 copy-start.7
  249.6 80.8 %all-to-all-start.2 = ((bf16[3,16,448,128]{3,2,0,1:T(8,128)(2,1)}), bf16[3,16,448,128]{3,2,0,1:T(8,128)(2,1)}, u32[]{:S(2)}, u32[]{:S(2)}) async-start(bf16[3,16,448,128]{3,2,0,1:T(8,128)(2,1)} %broadcast_in_dim.81), calls=%async_computation.2 | async-start | bytes 11010048 | tf_op jit(solution)/shard_map/all_to_all | solution.py:80
  254.5 242.5 %reduce-scatter.2.cloned.1.call-start = ((), (), s32[]{:S(2)}) async-start(), calls=%async_computation.7 | async-start | bytes 5849088 | tf_op jit(solution)/shard_map/reduce_scatter | solution.py:116
  262.8 4.2 copy-start
  262.8 5.3 copy-start.2
  262.8 2.9 copy-start.5
  264.1 4.0 copy-start.4
  341.0 2.6 copy-start.1
  346.9 203.0 %all-gather.4.cloned.1.call-start = ((), (), s32[]{:S(2)}) async-start(), calls=%async_computation.6 | async-start | bytes 5849088 | tf_op jit(solution)/shard_map/all_gather | solution.py:105
  498.8 14.0 %all-to-all-start.4 = ((bf16[16,16,448]{2,1,0:T(8,128)(2,1)}), bf16[16,16,448]{2,1,0:T(8,128)(2,1)S(1)}, u32[]{:S(2)}, u32[]{:S(2)}) async-start(bf16[16,16,448]{2,1,0:T(8,128)(2,1)} %bitcast.54), calls=%async_computation.5 | async-start | bytes 524288 | tf_op jit(solution)/shard_map/all_to_all | solution.py:121
Sparse Core Ops, SparseCore 0:
  43.0 185.9 all-gather.5
  347.0 122.4 reduce-scatter.1
  488.5 61.2 all-gather.3

commit v8 on v6

--- a/solution.py
+++ b/solution.py
@@ -1,3 +1,5 @@
+import functools
+
 import jax
 import jax.numpy as jnp
 from jax import lax
@@ -48,6 +50,24 @@
     return (gate_sum, up_sum, down_sum, back)
 
 
+def scatter_from(owner, own):
+    index = lax.axis_index("dp")
+    bits = own.shape[1].bit_length() - 1
+    held = own.reshape(own.shape[:1] + (2,) * bits + own.shape[2:])
+    axis_of = {bit: bits - bit for bit in range(bits)}
+    holders = {owner}
+    for bit in sorted(range(bits), key=lambda b: (b != 0, b == 1, b)):
+        axis = axis_of.pop(bit)
+        mine = (index >> bit) & 1
+        keep = lax.dynamic_index_in_dim(held, mine, axis=axis, keepdims=False)
+        send = lax.dynamic_index_in_dim(held, 1 - mine, axis=axis, keepdims=False)
+        got = lax.ppermute(send, "dp", [(h, h ^ (1 << bit)) for h in sorted(holders)])
+        held = jnp.where(((index ^ owner) >> bit) & 1 == 1, got, keep)
+        holders |= {h ^ (1 << bit) for h in holders}
+        axis_of = {b: a - (a > axis) for b, a in axis_of.items()}
+    return held.reshape(own.shape[:1] + own.shape[2:])
+
+
 def on_device(tokens, grad_out, w_gate, w_up, w_down, routing, combine, hot_ids):
     dp_count = lax.axis_size("dp")
     block_rows = tokens.shape[0]
@@ -74,8 +94,9 @@
     share_count = lax.axis_size("expert")
     own = jnp.stack([w_gate[0], w_up[0], w_down[0].T], 0)
     own = own.reshape(3, share_count, width // share_count, own.shape[-1])
-    pieces = lax.all_to_all(own, "dp", split_axis=1, concat_axis=1, tiled=True)
-    hot_piece = lax.dynamic_index_in_dim(pieces, hot_expert, axis=1, keepdims=False)
+    hot_piece = lax.switch(
+        hot_expert, [functools.partial(scatter_from, owner) for owner in range(dp_count)], own
+    )
     copies = jnp.broadcast_to(hot_piece[:, None], own.shape)
     hot_w = lax.all_to_all(copies, "dp", split_axis=1, concat_axis=1, tiled=True)
 

time: 534 us -> 511 us (0.957)
  waiting for transfers between devices: 260 us -> 207 us
  starting transfers between devices: 15.6 us -> 25.1 us
  loops' own time: 0 us -> 8.81 us
  other arithmetic: 29.1 us -> 37.7 us
    all_to_all x1 -> x0, waiting for transfers between devices: 122 us -> none  [on_device(): pieces = lax.all_to_all(own, 'dp', split_axis=1, concat_axis=1, tiled=True)]
    ppermute x0 -> x4, waiting for transfers between devices: none -> 55.8 us  [scatter_from(): got = lax.ppermute(send, 'dp', [(h, h ^ 1 << bit) for h in sorted(holders)])]
    all_gather x1, waiting for transfers between devices: 35.6 us -> 50.9 us  [on_device(): lax.all_gather(chunk_sum, 'dp', axis=1, tiled=True)]
    all_to_all x1, waiting for transfers between devices: 24.4 us -> 13.8 us  [on_device(): lax.all_to_all(copies, 'dp', split_axis=1, concat_axis=1, tiled=True)]
    all_gather x1, waiting for transfers between devices: 72.7 us -> 82.5 us  [on_device(): lax.all_gather(jnp.concatenate([grad_out, arrived_back], 0), 'expert', ax...]
    another operation x0 -> x1, loops' own time: none -> 8.81 us  [on_device(): lax.switch(hot_expert, [functools.partial(scatter_from, owner) for owner...]
    all_to_all x1, starting transfers between devices: 4.66 us -> 11.3 us  [on_device(): lax.all_to_all(cold_share.astype(jnp.bfloat16), 'dp', split_axis=0, conca...]
    select_n x0 -> x4, other arithmetic: none -> 6.63 us  [scatter_from(): held = jnp.where((index ^ owner) >> bit & 1 == 1, got, keep)]
  transfers between devices with their start and end apart: 7 -> 10, of which waited for: 5 -> 5; matrix products, arithmetic and copies ran while one was open for 12% -> 14% of each run, Pallas kernels for 0% -> 0%
where the time goes in v8:
time: 511 us; the launch traced here: 509 us
  waiting for transfers between devices  207 us (41%)
  blocking collectives  135 us (26%)
  matrix products  49.8 us (10%)
  other arithmetic  37.7 us (7%)
  local copies, waits for them, and re-layouts  30.9 us (6%)
  starting transfers between devices  25.1 us (5%)
  between operations  14.7 us (3%)
  loops' own time  8.81 us (2%)
    all_to_all x1, blocking collectives, on_device(): lax.all_to_all(block_sums, 'dp', split_axis=1, concat_axis=1, tiled=True)  116 us
    all_gather x1, waiting for transfers between devices, on_device(): lax.all_gather(jnp.concatenate([grad_out, arrived_back], 0), 'expert', ax...  82.5 us
    ppermute x4, waiting for transfers between devices, scatter_from(): got = lax.ppermute(send, 'dp', [(h, h ^ 1 << bit) for h in sorted(holders)])  55.8 us
    all_gather x1, waiting for transfers between devices, on_device(): lax.all_gather(chunk_sum, 'dp', axis=1, tiled=True)  50.9 us
    all_to_all x1, blocking collectives, on_device(): lax.all_to_all(packed, 'dp', split_axis=0, concat_axis=0, tiled=True)  18.9 us
    all_to_all x1, waiting for transfers between devices, on_device(): lax.all_to_all(copies, 'dp', split_axis=1, concat_axis=1, tiled=True)  13.8 us
    all_to_all x1, starting transfers between devices, on_device(): lax.all_to_all(cold_share.astype(jnp.bfloat16), 'dp', split_axis=0, conca...  11.3 us
  transfers between devices with their start and end apart: 10, of which 5 were waited for; matrix products, arithmetic and copies ran while one was open for 14% of the time, Pallas kernels for 0%

profile of v8, /device:TPU:1, one launch (start us, length us, event | category | flops | bytes accessed | tf_op | source)
XLA Modules:
  0.0 509.0 jit_solution(8908395878607375218)
XLA Ops:
  7.2 0.8 convert_reduce_fusion
  8.2 0.7 iota_compare_fusion.4
  8.8 4.5 select_reduce_fusion
  13.3 0.7 copy-done.21
  14.1 4.6 fusion.31
  18.7 1.0 copy.80
  19.7 1.0 copy.81
  20.7 1.2 gather_fusion.2
  21.9 1.2 gather_fusion.1
  23.4 18.9 %all_to_all.20 = bf16[16,16,896]{2,1,0:T(8,128)(2,1)S(1)} all-to-all(bf16[16,16,896]{2,1,0:T(8,128)(2,1)S(1)} %pad_maximum_fusion.3), channel_id=1, replica_groups=mesh['dp'=16,'expert'=16] {'dp'}, dimensions={0} | all-to-all | bytes 917504 | tf_op jit(solution)/shard_map/all_to_all | solution.py:110
  42.5 0.8 pad_maximum_fusion.4
  43.4 0.8 pad_maximum_fusion.5
  44.3 3.9 copy.87
  48.2 5.0 pad_maximum_fusion
  53.1 82.7 %conditional.1 = (bf16[3,448,128]{2,1,0:T(8,128)(2,1)}, s32[]{:T(128)}, s32[]{:T(128)}, s32[]{:T(128)}, s32[]{:T(128)}, /*index=5*/bf16[3,2,448,128]{3,2,1,0:T(8...) conditional(s32[]{:T(128)} %clamp.7, ...), branch_computations={%region_4.6_spmd, %region_5.7_spmd, %region_6.8_spmd, %region_7.9_... | conditional | flops 2408496 | bytes 52298636 | solution.py:97
  61.7 2.0 dynamic-slice_bitcast_fusion.60
  63.7 2.2 collective-permute-start.60
  66.0 2.1 bitcast_select_fusion.45
  68.1 1.2 dynamic-slice_bitcast_fusion.61
  69.2 1.7 collective-permute-start.61
  71.0 1.5 bitcast_select_fusion.46
  72.5 1.1 copy-done.19
  73.6 0.7 collective-permute-start.62
  74.3 2.0 bitcast_select_fusion.47
  76.4 1.0 dynamic-slice_bitcast_fusion.63
  77.4 1.3 collective-permute-start.63
  78.7 1.1 copy.302
  79.8 55.8 %collective-permute-done.63 = bf16[3,448,128]{2,1,0:T(8,128)(2,1)} collective-permute-done((bf16[3,448,128]{2,1,0:T(8,128)(2,1)S(1)}, bf16[3,448,128]{2,1,0:T(8,128)(2,1)}, u32[]{:S(2)}, u32[]{:S(2)}) %collective-permute-start.63) | collective-permute-done | bytes 344096 | tf_op jit(solution)/shard_map/cond/branch_15_fun/ppermute | solution.py:64
  135.8 1.0 bitcast_select_fusion.48
  136.8 3.7 broadcast_in_dim.78
  140.5 7.4 %all-to-all-start.1 = ((bf16[3,16,448,128]{3,2,0,1:T(8,128)(2,1)}), bf16[3,16,448,128]{3,2,0,1:T(8,128)(2,1)}, u32[]{:S(2)}, u32[]{:S(2)}) async-start(bf16[3,16,448,128]{3,2,0,1:T(8,128)(2,1)} %broadcast_in_dim.78), calls=%async_computation.1 | async-start | bytes 11010048 | tf_op jit(solution)/shard_map/all_to_all | solution.py:101
  148.1 0.9 constant_dynamic-slice_fusion
  149.3 2.4 gather_fusion
  151.8 3.6 fusion.41
  155.9 2.7 fusion.44
  158.6 82.5 %all-gather.10.cloned.1.call-done = bf16[6144,448]{1,0:T(8,128)(2,1)} async-done(((bf16[384,448]{1,0:T(8,128)(2,1)}), bf16[6144,448]{1,0:T(8,128)(2,1)}) %all-gather.10.cloned.1.call-update) | async-done | bytes 5505040 | tf_op jit(solution)/shard_map/all_gather | solution.py:114
  241.1 4.0 multiply_convert_fusion.2
  245.1 1.1 fusion.74
  246.3 3.0 fusion.5
  249.3 13.8 %all-to-all-done.1 = bf16[3,16,448,128]{3,2,0,1:T(8,128)(2,1)} async-done(((bf16[3,16,448,128]{3,2,0,1:T(8,128)(2,1)}), bf16[3,16,448,128]{3,2,0,1:T(8,128)(2,1)}, u32[]{:S(2)}, u32[]{:S(2)}) %all-to-all-start.1) | async-done | bytes 5505056 | tf_op jit(solution)/shard_map/all_to_all | solution.py:101
  263.1 2.8 fusion.54
  265.9 2.8 fusion.57
  268.7 2.8 multiply_convert_fusion.5
  271.6 2.1 fusion.33
  273.8 2.3 fusion.35
  276.3 3.2 pad_maximum_fusion.2
  279.8 2.3 convert_bitcast_fusion.2
  282.2 2.3 convert_bitcast_fusion.1
  284.5 2.4 convert_bitcast_fusion
  286.9 0.9 pad_maximum_fusion.1
  288.2 116.0 %all_to_all.21 = bf16[3,16,448,128]{3,2,0,1:T(8,128)(2,1)} all-to-all(bf16[3,16,448,128]{3,2,0,1:T(8,128)(2,1)S(1)} %copy.91), channel_id=1, replica_groups=mesh['dp'=16,'expert'=16] {'dp'}, dimensions={1} | all-to-all | bytes 11010048 | tf_op jit(solution)/shard_map/all_to_all | solution.py:121
  404.2 4.3 reduce_sum.42
  408.7 3.6 fusion.19
  412.3 4.9 fusion.22
  417.2 1.0 slice.105
  418.2 0.8 copy.95
  419.0 11.3 %all-to-all-start.3 = ((bf16[16,16,448]{2,1,0:T(8,128)(2,1)}), bf16[16,16,448]{2,1,0:T(8,128)(2,1)S(1)}, u32[]{:S(2)}, u32[]{:S(2)}) async-start(bf16[16,16,448]{2,1,0:T(8,128)(2,1)} %bitcast.178), calls=%async_computation.4 | async-start | bytes 524288 | tf_op jit(solution)/shard_map/all_to_all | solution.py:139
  430.4 4.8 fusion.16
  435.2 4.0 all-to-all-done.3
  439.2 1.8 fusion.40
  441.0 50.9 %all-gather.6.cloned.1.call-done = bf16[3,7168,128]{2,1,0:T(8,128)(2,1)} async-done(((bf16[3,448,128]{2,1,0:T(8,128)(2,1)}), bf16[3,7168,128]{2,1,0:T(8,128)(2,1)}) %all-gather.6.cloned.1.call-update) | async-done | bytes 5505040 | tf_op jit(solution)/shard_map/all_gather | solution.py:123
  491.9 5.1 fusion
  497.0 2.2 fusion.96
  499.2 2.9 copy.94
  (59 shorter events, 3.1 us)
Async XLA Ops:
  7.2 144.6 %all-gather.8.cloned.1.call-start = ((), (), s32[]{:S(2)}) async-start(), calls=%async_computation.7 | async-start | bytes 6684672 | tf_op jit(solution)/shard_map/all_gather | solution.py:113
  13.3 0.7 copy-start.21
  14.1 4.6 copy-start.24
  23.3 21.0 %copy-start.26 = (s32[16]{0:T(128)S(1)}, s32[16]{0:T(128)}, u32[]{:S(2)}) copy-start(s32[16]{0:T(128)} %param.33) | copy-start | bytes 196
  43.3 4.9 copy-start.2
  43.3 197.8 %all-gather.10.cloned.1.call-start = ((), (), s32[]{:S(2)}) async-start(), calls=%async_computation.8 | async-start | bytes 6684672 | tf_op jit(solution)/shard_map/all_gather | solution.py:114
  63.7 2.2 collective-permute-start.60
  69.2 1.7 collective-permute-start.61
  72.5 1.1 copy-start.19
  73.6 0.7 collective-permute-start.62
  77.4 58.2 %collective-permute-start.63 = (bf16[3,448,128]{2,1,0:T(8,128)(2,1)S(1)}, bf16[3,448,128]{2,1,0:T(8,128)(2,1)}, u32[]{:S(2)}, u32[]{:S(2)}) collective-permute-start(bf16[3,448,128]{2,1,0:T(8,128)(2,1)S(1)} %dynamic-slice_bitcast_fusion.63), channel_id=1, source_target_pairs={{32,0},{48,16},{96,64},{112,80},{160,128},{176,144},{224,192},{240... | collective-permute-start | bytes 1032200 | tf_op jit(solution)/shard_map/cond/branch_15_fun/ppermute | solution.py:64
  140.5 8.7 %copy-start.22 = (s32[2048,2]{0,1:T(2,128)S(1)}, s32[2048,2]{0,1:T(2,128)}, u32[]{:S(2)}) copy-start(s32[2048,2]{0,1:T(2,128)} %param.31) | copy-start | bytes 49156
  140.5 8.8 %copy-start.23 = (f32[2048,2]{0,1:T(2,128)S(1)}, f32[2048,2]{0,1:T(2,128)}, u32[]{:S(2)}) copy-start(f32[2048,2]{0,1:T(2,128)} %param.32) | copy-start | bytes 49156
  140.5 122.6 %all-to-all-start.1 = ((bf16[3,16,448,128]{3,2,0,1:T(8,128)(2,1)}), bf16[3,16,448,128]{3,2,0,1:T(8,128)(2,1)}, u32[]{:S(2)}, u32[]{:S(2)}) async-start(bf16[3,16,448,128]{3,2,0,1:T(8,128)(2,1)} %broadcast_in_dim.78), calls=%async_computation.1 | async-start | bytes 11010048 | tf_op jit(solution)/shard_map/all_to_all | solution.py:101
  147.9 269.3 %reduce-scatter.2.cloned.1.call-start = ((), (), s32[]{:S(2)}) async-start(), calls=%async_computation.6 | async-start | bytes 5849088 | tf_op jit(solution)/shard_map/reduce_scatter | solution.py:134
  149.3 2.5 copy-start.3
  151.8 4.2 copy-start
  241.1 4.1 copy-start.4
  273.8 2.6 copy-start.1
  279.5 212.4 %all-gather.6.cloned.1.call-start = ((), (), s32[]{:S(2)}) async-start(), calls=%async_computation.5 | async-start | bytes 5849088 | tf_op jit(solution)/shard_map/all_gather | solution.py:123
  419.0 20.2 %all-to-all-start.3 = ((bf16[16,16,448]{2,1,0:T(8,128)(2,1)}), bf16[16,16,448]{2,1,0:T(8,128)(2,1)S(1)}, u32[]{:S(2)}, u32[]{:S(2)}) async-start(bf16[16,16,448]{2,1,0:T(8,128)(2,1)} %bitcast.178), calls=%async_computation.4 | async-start | bytes 524288 | tf_op jit(solution)/shard_map/all_to_all | solution.py:139
  430.3 8.9 %copy-start.25 = (s32[256]{0:T(256)S(1)}, s32[256]{0:T(256)}, u32[]{:S(2)}) copy-start(s32[256]{0:T(256)} %copy-done.24) | copy-start | bytes 3076
Sparse Core Ops, SparseCore 0:
  43.4 76.8 all-gather.7
  122.1 118.9 all-gather.9
  279.7 133.9 reduce-scatter.1
  416.8 75.0 all-gather.5
